TPU v7x, 256 devices: a whole 4x4x8 slice. The times are simulated.
256 devices in a mesh: dp: 4 (over y), expert: 64 (over z, x, core).
Axes of the slice: x: 4, y: 4, z: 8, core: 2. Of those that a mesh axis runs over, the one named last changes fastest.
Arguments:
- tokens: bfloat16 [8192, 2048], P(('dp', 'expert')), may hold values from -6 to 6
- routes: int32 [8192, 8], P(('dp', 'expert')), may hold values from 0 to 63, all different within a row; in each aligned block of 32 rows (0 to 31, 32 to 63, ...) at most 6 rows name the same one
- gates: float32 [8192, 8], P(('dp', 'expert')), may hold values from 0.1 to 0.6
- w_gate: bfloat16 [64, 2048, 768], P('expert'), may hold values from -0.125 to 0.125
- w_up: bfloat16 [64, 2048, 768], P('expert'), may hold values from -0.125 to 0.125
- w_down: bfloat16 [64, 768, 2048], P('expert'), may hold values from -0.21875 to 0.21875
- swap_flags: int32 [64], replicated, may hold values from 0 to 1, as said below
- d_out: bfloat16 [8192, 2048], P(('dp', 'expert')), may hold values from -6 to 6
Outputs:
- mixture: bfloat16 [8192, 2048], P(('dp', 'expert'))
- d_tokens: bfloat16 [8192, 2048], P(('dp', 'expert'))
- d_gates: float32 [8192, 8], P(('dp', 'expert'))
- g_gate: bfloat16 [64, 2048, 768], P('expert', 'dp')
- g_up: bfloat16 [64, 2048, 768], P('expert', 'dp')
- g_down: bfloat16 [64, 768, 2048], P('expert', None, 'dp')
Inputs may be any that keep to these rules, and one draw needn't show every extreme that they name: `routes`: among the 32 rows of one device no expert is named more than 6 times, and in every draw some device names some expert exactly 6 times. swap_flags[i] equals swap_flags[i + 32]; swap_flags[0] and swap_flags[31] are 1.
All inputs are finite; a program needn't handle non-finite values.
Results may differ from a plain program's by a relative error of at most 0.0095.
Values may be sent and summed in bfloat16 or wider, within the bound.
No kernel may reach another device: no remote copies, remote signals or barrier semaphores. Data moves between devices by JAX's collectives and lax.ppermute only.
A program may use at most 128 MiB of HBM per device.

v0:
```python
import jax
import jax.numpy as jnp
from jax import lax
from jax.sharding import Mesh, PartitionSpec as P


N_Z, N_X, N_CORE = 8, 4, 2
PLANE = ("x", "core")
BF16, F32 = jnp.bfloat16, jnp.float32


def dot(left, right, lc=1, rc=0):
    return lax.dot_general(left, right, (((lc,), (rc,)), ((), ())), preferred_element_type=F32)


def split3(value):
    first = lax.reduce_precision(value, 8, 7)
    second = lax.reduce_precision(value - first, 8, 7)
    third = value - first - second
    return [part.astype(BF16) for part in (first, second, third)]


def padded(parts, width):
    used = sum(p.shape[1] for p in parts)
    return jnp.concatenate(parts + [jnp.zeros((parts[0].shape[0], width - used), BF16)], axis=1)


def on_device(tokens, routes, gates, w_gate, w_up, w_down, swap_flags, d_out):
    tok_count, model_width = tokens.shape
    top_count = routes.shape[1]
    plane = N_X * N_CORE
    experts = N_Z * plane
    capacity = min(tok_count, (3 * tok_count * top_count + 2 * experts - 1) // (2 * experts))
    column = N_Z * tok_count
    per_expert = N_Z * capacity
    slots = plane * per_expert
    z_index = lax.axis_index("z")
    own_index = (z_index * N_X + lax.axis_index("x")) * N_CORE + lax.axis_index("core")
    own_flag = swap_flags[own_index]
    gate_mat, up_mat, down_mat = w_gate[0], w_up[0], w_down[0]

    meta = padded([routes.astype(BF16)] + split3(gates), 128)
    gathered = lax.all_gather(jnp.concatenate([tokens, d_out, meta], axis=1), "z", tiled=True)
    tok_col = gathered[:, :model_width]
    dout_col = gathered[:, model_width : 2 * model_width]
    meta_col = gathered[:, 2 * model_width : 2 * model_width + 4 * top_count].astype(F32)
    routes_col = meta_col[:, :top_count].astype(jnp.int32)
    gates_col = (
        meta_col[:, top_count : 2 * top_count]
        + meta_col[:, 2 * top_count : 3 * top_count]
        + meta_col[:, 3 * top_count :]
    )

    block = jnp.arange(experts, dtype=jnp.int32)
    block_expert = block % N_Z * plane + block // N_Z
    sent = jnp.any(routes[:, None, :] == block_expert[None, :, None], axis=2)
    own_row = jnp.arange(tok_count, dtype=jnp.int32)
    own_position = dot(
        (own_row[:, None] > own_row[None, :]).astype(BF16), sent.astype(BF16)
    ).astype(jnp.int32)
    own_pick = jnp.where(sent, own_position, -1).T[:, None, :] == jnp.arange(
        capacity, dtype=jnp.int32
    )[None, :, None]
    own_pick = own_pick.reshape(slots, tok_count).astype(BF16)
    outbound = dot(own_pick, tokens).astype(BF16).reshape(experts, capacity, model_width)
    rows_in = lax.all_to_all(
        outbound, ("x", "core", "z"), split_axis=0, concat_axis=0, tiled=True
    ).reshape(slots, model_width)

    row = jnp.arange(column, dtype=jnp.int32)
    earlier = (
        (row[:, None] > row[None, :])
        & (row[:, None] // tok_count == row[None, :] // tok_count)
    ).astype(BF16)
    slot_ids = jnp.arange(slots, dtype=jnp.int32).reshape(plane, per_expert)

    def selection(ids):
        named = routes_col[:, None, :] == ids[None, :, None]
        member = jnp.any(named, axis=2)
        gate_of = jnp.sum(jnp.where(named, gates_col[:, None, :], 0.0), axis=2)
        position = dot(earlier, member.astype(BF16)).astype(jnp.int32)
        slot_of = jnp.where(
            member,
            jnp.arange(plane, dtype=jnp.int32)[None, :] * per_expert
            + (row // tok_count)[:, None] * capacity
            + position,
            -1,
        )
        pick = slot_of.T[:, None, :] == slot_ids[:, :, None]
        slot_gate = jnp.sum(jnp.where(pick, gate_of.T[:, None, :], 0.0), axis=2)
        return pick.astype(BF16).reshape(slots, column), slot_gate.reshape(slots, 1)

    def to_plane(rows):
        rows = rows.reshape(plane, per_expert, -1)
        rows = lax.all_to_all(rows, PLANE, split_axis=0, concat_axis=0, tiled=True)
        return rows.reshape(slots, -1)

    def to_column(rows):
        rows = rows.reshape(N_Z, tok_count, -1)
        return lax.all_to_all(rows, "z", split_axis=0, concat_axis=0, tiled=True)

    def token_rows(pick):
        rows = dot(pick, tok_col).astype(BF16)
        return to_plane(rows)

    def cot_pairs(pick, slot_gate):
        rows = (slot_gate * dot(pick, dout_col)).astype(BF16)
        return to_plane(rows)

    plane_ids = z_index * plane + jnp.arange(plane, dtype=jnp.int32)
    pick, slot_gate = selection(plane_ids)
    cot_rows = cot_pairs(pick, slot_gate)

    plane_flags = lax.dynamic_slice(swap_flags, (z_index * plane,), (plane,))
    placed_pick, placed_gate = selection(
        jnp.where(plane_flags == 1, plane_ids ^ (experts // 2), plane_ids)
    )
    placed_cot = cot_pairs(placed_pick, placed_gate)
    placed_tok = token_rows(placed_pick)

    pre_gate = dot(rows_in, gate_mat)
    pre_up = dot(rows_in, up_mat)
    logistic = jax.nn.sigmoid(pre_gate)
    activated = pre_gate * logistic
    hidden = (activated * pre_up).astype(BF16)
    _, cot_rows = lax.optimization_barrier((hidden, cot_rows))
    d_hidden = dot(cot_rows, down_mat, 1, 1)
    grad_gate_pre = (d_hidden * pre_up * logistic * (1.0 + pre_gate * (1.0 - logistic))).astype(
        BF16
    )
    grad_up_pre = (d_hidden * activated).astype(BF16)
    result = dot(hidden, down_mat).astype(BF16)
    d_rows = (dot(grad_gate_pre, gate_mat, 1, 1) + dot(grad_up_pre, up_mat, 1, 1)).astype(BF16)

    def placed(own):
        other = lax.ppermute(own, "z", [(i, i ^ (N_Z // 2)) for i in range(N_Z)])
        return jnp.where(own_flag == 1, other, own)

    def reduced(left, right):
        partial = dot(left, right, 0, 0).astype(BF16)
        return lax.psum_scatter(partial, "dp", scatter_dimension=0, tiled=True)

    g_down = reduced(placed_cot, placed(hidden)).T[None]
    g_gate = reduced(placed_tok, placed(grad_gate_pre))[None]
    g_up = reduced(placed_tok, placed(grad_up_pre))[None]

    out_rows = to_plane(result)
    weight = jnp.where(
        pick == 1, jnp.broadcast_to(slot_gate, pick.shape), 0.0
    )
    weight_hi = lax.reduce_precision(weight, 8, 7)
    weight_lo = (weight - weight_hi).astype(BF16)
    mix_part = dot(weight_hi.astype(BF16), out_rows, 0, 0) + dot(weight_lo, out_rows, 0, 0)
    cross = dot(dout_col, out_rows, 1, 1)
    slot_expert = z_index * plane + jnp.arange(slots, dtype=jnp.int32) // per_expert
    cross = cross * pick.T.astype(F32)
    dg_part = jnp.sum(
        jnp.where(routes_col[:, :, None] == slot_expert[None, None, :], cross[:, None, :], 0.0),
        axis=2,
    )
    parts = to_column(
        jnp.concatenate([mix_part.astype(BF16), padded(split3(dg_part), 128)], axis=1),
    )
    mixture = jnp.sum(parts[:, :, :model_width].astype(F32), axis=0).astype(BF16)
    dg_sum = jnp.sum(parts[:, :, model_width : model_width + 3 * top_count].astype(F32), axis=0)
    d_gates = (
        dg_sum[:, :top_count]
        + dg_sum[:, top_count : 2 * top_count]
        + dg_sum[:, 2 * top_count :]
    )
    back_rows = to_plane(d_rows)
    d_tokens = jnp.sum(
        to_column(dot(pick, back_rows, 0, 0).astype(BF16)).astype(F32), axis=0
    ).astype(BF16)
    return (mixture, d_tokens, d_gates, g_gate, g_up, g_down)


def solution(mesh):
    fine = Mesh(mesh.devices.reshape(-1, N_Z, N_X, N_CORE), ("dp", "z", "x", "core"))
    every = ("dp", "z", "x", "core")
    expert = ("z", "x", "core")
    return jax.shard_map(
        on_device,
        mesh=fine,
        in_specs=(
            P(every, None),
            P(every, None),
            P(every, None),
            P(expert, None, None),
            P(expert, None, None),
            P(expert, None, None),
            P(),
            P(every, None),
        ),
        out_specs=(
            P(every, None),
            P(every, None),
            P(every, None),
            P(expert, "dp", None),
            P(expert, "dp", None),
            P(expert, None, "dp"),
        ),
        check_vma=False,
    )
```

profile of v0, /device:TPU:1, one launch (start us, length us, event | category | flops | bytes accessed | tf_op | source)
XLA Modules:
  0.0 376.2 jit_solution(6837782834875018514)
XLA Ops:
  7.2 0.8 convert_element_type.117
  8.2 0.7 fusion.67
  9.2 1.8 concatenate.6
  11.0 0.8 copy.56
  12.0 0.7 copy.57
  12.7 0.8 eq.167
  13.5 0.7 eq.168
  14.2 0.1 eq.170
  14.3 2.7 convolution_convert_fusion.3
  17.0 3.7 reshape.243
  20.7 13.3 %all-to-all-start = ((bf16[64,6,2048]{2,1,0:T(8,128)(2,1)}), bf16[64,6,2048]{2,1,0:T(8,128)(2,1)}, u32[]{:S(2)}, u32[]{:S(2)}) async-start(bf16[64,6,2048]{2,1,0:T(8,128)(2,1)} %reshape.243), calls=%async_computation | async-start | bytes 4194304 | tf_op jit(solution)/shard_map/all_to_all | solution.py:66
  34.2 63.8 %all-to-all-done = bf16[64,6,2048]{2,1,0:T(8,128)(2,1)} async-done(((bf16[64,6,2048]{2,1,0:T(8,128)(2,1)}), bf16[64,6,2048]{2,1,0:T(8,128)(2,1)}, u32[]{:S(2)}, u32[]{:S(2)}) %all-to-all-start) | async-done | bytes 1572896 | tf_op jit(solution)/shard_map/all_to_all | solution.py:66
  98.0 3.7 reshape.244
  101.7 0.8 slice_convert_fusion.1
  102.6 0.2 slice_convert_fusion
  103.0 0.7 fusion.65
  103.7 0.2 fusion.23
  104.0 0.2 fusion.25
  104.2 0.3 copy-done.7
  104.6 0.9 copy.64
  105.6 0.9 copy.58
  106.5 1.0 select_reduce_fusion.1
  107.6 1.2 broadcast_compare_fusion
  108.8 3.0 multiply_convert_fusion
  111.8 4.6 %all-to-all-start.7 = ((bf16[8,48,2048]{2,1,0:T(8,128)(2,1)}), bf16[8,48,2048]{2,1,0:T(8,128)(2,1)}, u32[]{:S(2)}, u32[]{:S(2)}) async-start(bf16[8,48,2048]{2,1,0:T(8,128)(2,1)} %bitcast.86), calls=%async_computation.9 | async-start | bytes 3145728 | tf_op jit(solution)/shard_map/all_to_all | solution.py:95
  116.4 3.9 %fusion.10 = f32[384,768]{1,0:T(8,128)S(1)} fusion(bf16[384,2048]{1,0:T(8,128)(2,1)} %reshape.244, bf16[1,2048,768]{2,1,0:T(8,128)(2,1)} %param.11), kind=kOutput, calls=%fused_computation.13 | convolution fusion | flops 1207959552 | bytes 5898240 | tf_op jit(solution)/shard_map/dot_general | solution.py:13
  120.3 2.6 multiply_convert_fusion.4
  123.0 2.8 collective-permute-start.2
  125.8 0.6 dynamic_slice.7
  127.0 15.1 %collective-permute-done.2 = bf16[384,768]{1,0:T(8,128)(2,1)} collective-permute-done((bf16[384,768]{1,0:T(8,128)(2,1)}, bf16[384,768]{1,0:T(8,128)(2,1)}, u32[]{:S(2)}, u32[]{:S(2)}) %collective-permute-start.2) | collective-permute-done | bytes 589856 | tf_op jit(solution)/shard_map/ppermute | solution.py:136
  142.1 5.0 %convolution_convert_fusion = bf16[2048,768]{1,0:T(8,128)(2,1)} fusion(bf16[384,2048]{1,0:T(8,128)(2,1)} %bitcast.27, bf16[384,768]{1,0:T(8,128)(2,1)} %collective-permute-done.2, bf16[384,768]{1,0:T(8,128)(2,1)} %get-tuple-element.56, pred[]{:T(512)} %bitcast.22), kind=kOutput, calls=%fused_computation | convolution fusion | flops 1209827328 | bytes 5898241 | tf_op jit(solution)/shard_map/dot_general | solution.py:13
  147.2 3.0 multiply_convert_fusion.1
  150.2 5.5 %all-to-all-start.3 = ((bf16[8,48,2048]{2,1,0:T(8,128)(2,1)}), bf16[8,48,2048]{2,1,0:T(8,128)(2,1)}, u32[]{:S(2)}, u32[]{:S(2)}) async-start(bf16[8,48,2048]{2,1,0:T(8,128)(2,1)} %bitcast.89), calls=%async_computation.3 | async-start | bytes 3145728 | tf_op jit(solution)/shard_map/all_to_all | solution.py:95
  155.8 3.0 convolution_convert_fusion.4
  158.7 17.7 %all-to-all-done.3 = bf16[8,48,2048]{2,1,0:T(8,128)(2,1)} async-done(((bf16[8,48,2048]{2,1,0:T(8,128)(2,1)}), bf16[8,48,2048]{2,1,0:T(8,128)(2,1)}, u32[]{:S(2)}, u32[]{:S(2)}) %all-to-all-start.3) | async-done | bytes 1572896 | tf_op jit(solution)/shard_map/all_to_all | solution.py:95
  176.4 5.2 %all-to-all-start.6 = ((bf16[8,48,2048]{2,1,0:T(8,128)(2,1)}), bf16[8,48,2048]{2,1,0:T(8,128)(2,1)}, u32[]{:S(2)}, u32[]{:S(2)}) async-start(bf16[8,48,2048]{2,1,0:T(8,128)(2,1)} %bitcast.85), calls=%async_computation.6 | async-start | bytes 3145728 | tf_op jit(solution)/shard_map/all_to_all | solution.py:95
  181.6 4.9 %multiply_convert_fusion.3 = (bf16[384,768]{1,0:T(8,128)(2,1)}, bf16[384,768]{1,0:T(8,128)(2,1)}) fusion(f32[384,768]{1,0:T(8,128)} %copy-done.13, f32[384,768]{1,0:T(8,128)} %get-tuple-element.57, bf16[384,2048]{1,0:T(8,128)(2,1)} %bitcast.14, bf16[1,768,2048]{2,1,0:T(8,128)(2,1)S(1)} %copy-done), kind=kOutput, calls=%fused_computation.30 | convolution fusion | flops 1211793408 | bytes 8257536 | tf_op jit(solution)/shard_map/dot_general | solution.py:13
  186.5 2.8 collective-permute-start
  189.3 13.1 %all-to-all-done.6 = bf16[8,48,2048]{2,1,0:T(8,128)(2,1)} async-done(((bf16[8,48,2048]{2,1,0:T(8,128)(2,1)}), bf16[8,48,2048]{2,1,0:T(8,128)(2,1)}, u32[]{:S(2)}, u32[]{:S(2)}) %all-to-all-start.6) | async-done | bytes 1572896 | tf_op jit(solution)/shard_map/all_to_all | solution.py:95
  202.3 3.0 collective-permute-done
  205.3 5.0 %convolution_convert_fusion.2 = bf16[2048,768]{1,0:T(8,128)(2,1)} fusion(bf16[384,2048]{1,0:T(8,128)(2,1)} %bitcast.21, bf16[384,768]{1,0:T(8,128)(2,1)} %collective-permute-done, bf16[384,768]{1,0:T(8,128)(2,1)} %get-tuple-element.44, pred[]{:T(512)} %bitcast.22), kind=kOutput, calls=%fused_computation.2 | convolution fusion | flops 1209827328 | bytes 5898241 | tf_op jit(solution)/shard_map/dot_general | solution.py:13
  210.4 2.8 collective-permute-start.1
  213.2 3.6 fusion.14
  216.8 6.1 %all-to-all-start.1 = ((bf16[8,48,2048]{2,1,0:T(8,128)(2,1)}), bf16[8,48,2048]{2,1,0:T(8,128)(2,1)S(1)}, u32[]{:S(2)}, u32[]{:S(2)}) async-start(bf16[8,48,2048]{2,1,0:T(8,128)(2,1)} %bitcast.88), calls=%async_computation.1 | async-start | bytes 3145728 | tf_op jit(solution)/shard_map/all_to_all | solution.py:95
  222.9 10.9 %collective-permute-done.1 = bf16[384,768]{1,0:T(8,128)(2,1)} collective-permute-done((bf16[384,768]{1,0:T(8,128)(2,1)}, bf16[384,768]{1,0:T(8,128)(2,1)}, u32[]{:S(2)}, u32[]{:S(2)}) %collective-permute-start.1) | collective-permute-done | bytes 589856 | tf_op jit(solution)/shard_map/ppermute | solution.py:136
  233.8 5.0 %convolution_convert_fusion.1 = bf16[2048,768]{1,0:T(8,128)(2,1)} fusion(bf16[384,2048]{1,0:T(8,128)(2,1)} %bitcast.21, bf16[384,768]{1,0:T(8,128)(2,1)} %collective-permute-done.1, bf16[384,768]{1,0:T(8,128)(2,1)S(1)} %copy-done.12, pred[]{:T(512)} %bitcast.22), kind=kOutput, calls=%fused_computation.1 | convolution fusion | flops 1209827328 | bytes 5898241 | tf_op jit(solution)/shard_map/dot_general | solution.py:13
  238.9 3.5 fusion.4
  242.3 3.7 add_convert_fusion
  246.1 5.2 %all-to-all-start.4 = ((bf16[8,48,2048]{2,1,0:T(8,128)(2,1)}), bf16[8,48,2048]{2,1,0:T(8,128)(2,1)S(1)}, u32[]{:S(2)}, u32[]{:S(2)}) async-start(bf16[8,48,2048]{2,1,0:T(8,128)(2,1)} %bitcast.87), calls=%async_computation.4 | async-start | bytes 3145728 | tf_op jit(solution)/shard_map/all_to_all | solution.py:95
  251.3 2.0 convolution_multiply_fusion
  253.3 0.9 select_reduce_fusion
  254.6 0.9 convolution_bitcast_fusion.1
  255.5 1.8 fusion.18
  257.4 3.1 concatenate.7
  260.4 11.4 %all-to-all-done.4 = bf16[8,48,2048]{2,1,0:T(8,128)(2,1)S(1)} async-done(((bf16[8,48,2048]{2,1,0:T(8,128)(2,1)}), bf16[8,48,2048]{2,1,0:T(8,128)(2,1)S(1)}, u32[]{:S(2)}, u32[]{:S(2)}) %all-to-all-start.4) | async-done | bytes 1572896 | tf_op jit(solution)/shard_map/all_to_all | solution.py:95
  271.8 29.4 %all-to-all-start.2 = ((bf16[8,32,2176]{2,1,0:T(8,128)(2,1)}), bf16[8,32,2176]{2,1,0:T(8,128)(2,1)S(1)}, u32[]{:S(2)}, u32[]{:S(2)}) async-start(bf16[8,32,2176]{2,1,0:T(8,128)(2,1)} %bitcast.12), calls=%async_computation.2 | async-start | bytes 2228224 | tf_op jit(solution)/shard_map/all_to_all | solution.py:100
  301.2 1.8 fusion.19
  303.0 28.8 %all-to-all-done.2 = bf16[8,32,2176]{2,1,0:T(8,128)(2,1)S(1)} async-done(((bf16[8,32,2176]{2,1,0:T(8,128)(2,1)}), bf16[8,32,2176]{2,1,0:T(8,128)(2,1)S(1)}, u32[]{:S(2)}, u32[]{:S(2)}) %all-to-all-start.2) | async-done | bytes 1114144 | tf_op jit(solution)/shard_map/all_to_all | solution.py:100
  331.8 4.3 %all-to-all-start.5 = ((bf16[8,32,2048]{2,1,0:T(8,128)(2,1)}), bf16[8,32,2048]{2,1,0:T(8,128)(2,1)}, u32[]{:S(2)}, u32[]{:S(2)}) async-start(bf16[8,32,2048]{2,1,0:T(8,128)(2,1)} %bitcast.92), calls=%async_computation.5 | async-start | bytes 2097152 | tf_op jit(solution)/shard_map/all_to_all | solution.py:100
  336.2 0.7 copy.65
  336.9 2.2 slice_reduce_fusion
  339.1 26.2 %all-to-all-done.5 = bf16[8,32,2048]{2,1,0:T(8,128)(2,1)} async-done(((bf16[8,32,2048]{2,1,0:T(8,128)(2,1)}), bf16[8,32,2048]{2,1,0:T(8,128)(2,1)}, u32[]{:S(2)}, u32[]{:S(2)}) %all-to-all-start.5) | async-done | bytes 1048608 | tf_op jit(solution)/shard_map/all_to_all | solution.py:100
  365.3 2.1 reduce_sum.82
  367.4 2.3 copy.66
  (71 shorter events, 2.0 us)
Async XLA Ops:
  7.2 174.4 %copy-start = (bf16[1,768,2048]{2,1,0:T(8,128)(2,1)S(1)}, bf16[1,768,2048]{2,1,0:T(8,128)(2,1)}, u32[]{:S(2)}) copy-start(bf16[1,768,2048]{2,1,0:T(8,128)(2,1)} %param.13) | copy-start | bytes 9437188
  7.2 7.1 %copy-start.6 = (bf16[32,2048]{1,0:T(8,128)(2,1)S(1)}, bf16[32,2048]{1,0:T(8,128)(2,1)}, u32[]{:S(2)}) copy-start(bf16[32,2048]{1,0:T(8,128)(2,1)} %param.8) | copy-start | bytes 393220
  7.2 94.5 %all-gather.2.cloned.1.call-start = ((), (), s32[]{:S(2)}) async-start(), calls=%async_computation.11 | async-start | bytes 2433024 | tf_op jit(solution)/shard_map/all_gather | solution.py:43
  20.7 13.4 %copy-start.8 = (s32[64]{0:T(128)S(1)}, s32[64]{0:T(128)}, u32[]{:S(2)}) copy-start(s32[64]{0:T(128)} %param.14) | copy-start | bytes 772
  20.7 77.3 %all-to-all-start = ((bf16[64,6,2048]{2,1,0:T(8,128)(2,1)}), bf16[64,6,2048]{2,1,0:T(8,128)(2,1)}, u32[]{:S(2)}, u32[]{:S(2)}) async-start(bf16[64,6,2048]{2,1,0:T(8,128)(2,1)} %reshape.243), calls=%async_computation | async-start | bytes 4194304 | tf_op jit(solution)/shard_map/all_to_all | solution.py:66
  102.7 1.2 copy-start.4
  104.0 0.6 copy-start.7
  111.8 30.3 %all-to-all-start.7 = ((bf16[8,48,2048]{2,1,0:T(8,128)(2,1)}), bf16[8,48,2048]{2,1,0:T(8,128)(2,1)}, u32[]{:S(2)}, u32[]{:S(2)}) async-start(bf16[8,48,2048]{2,1,0:T(8,128)(2,1)} %bitcast.86), calls=%async_computation.9 | async-start | bytes 3145728 | tf_op jit(solution)/shard_map/all_to_all | solution.py:95
  116.4 251.0 %reduce-scatter.8.cloned.1.call-start = ((), (), s32[]{:S(2)}) async-start(), calls=%async_computation.14 | async-start | bytes 3932160 | tf_op jit(solution)/shard_map/reduce_scatter | solution.py:141
  116.4 3.9 %copy-start.3 = (bf16[384,2048]{1,0:T(8,128)(2,1)S(1)}, bf16[384,2048]{1,0:T(8,128)(2,1)}, u32[]{:S(2)}) copy-start(bf16[384,2048]{1,0:T(8,128)(2,1)} %reshape.244) | copy-start | bytes 4718596
  116.4 3.9 %copy-start.10 = (bf16[1,2048,768]{2,1,0:T(8,128)(2,1)S(1)}, bf16[1,2048,768]{2,1,0:T(8,128)(2,1)}, u32[]{:S(2)}) copy-start(bf16[1,2048,768]{2,1,0:T(8,128)(2,1)} %param.12) | copy-start | bytes 9437188
  120.3 2.6 copy-start.13
  120.3 5.5 %copy-start.9 = (s32[64]{0:T(128)S(1)}, s32[64]{0:T(128)}, u32[]{:S(2)}) copy-start(s32[64]{0:T(128)} %param.14) | copy-start | bytes 772
  123.0 19.1 %collective-permute-start.2 = (bf16[384,768]{1,0:T(8,128)(2,1)}, bf16[384,768]{1,0:T(8,128)(2,1)}, u32[]{:S(2)}, u32[]{:S(2)}) collective-permute-start(bf16[384,768]{1,0:T(8,128)(2,1)} %get-tuple-element.56), channel_id=1, source_target_pairs={{0,32},{8,40},{16,48},{24,56},{32,0},{40,8},{48,16},{56,24},{1,33}... | collective-permute-start | bytes 1769480 | tf_op jit(solution)/shard_map/ppermute | solution.py:136
  150.2 26.2 %all-to-all-start.3 = ((bf16[8,48,2048]{2,1,0:T(8,128)(2,1)}), bf16[8,48,2048]{2,1,0:T(8,128)(2,1)}, u32[]{:S(2)}, u32[]{:S(2)}) async-start(bf16[8,48,2048]{2,1,0:T(8,128)(2,1)} %bitcast.89), calls=%async_computation.3 | async-start | bytes 3145728 | tf_op jit(solution)/shard_map/all_to_all | solution.py:95
  176.4 25.9 %all-to-all-start.6 = ((bf16[8,48,2048]{2,1,0:T(8,128)(2,1)}), bf16[8,48,2048]{2,1,0:T(8,128)(2,1)}, u32[]{:S(2)}, u32[]{:S(2)}) async-start(bf16[8,48,2048]{2,1,0:T(8,128)(2,1)} %bitcast.85), calls=%async_computation.6 | async-start | bytes 3145728 | tf_op jit(solution)/shard_map/all_to_all | solution.py:95
  181.6 188.1 %reduce-scatter.4.cloned.1.call-start = ((), (), s32[]{:S(2)}) async-start(), calls=%async_computation.12 | async-start | bytes 3932160 | tf_op jit(solution)/shard_map/reduce_scatter | solution.py:141
  186.5 18.8 %collective-permute-start = (bf16[384,768]{1,0:T(8,128)(2,1)}, bf16[384,768]{1,0:T(8,128)(2,1)}, u32[]{:S(2)}, u32[]{:S(2)}) collective-permute-start(bf16[384,768]{1,0:T(8,128)(2,1)} %get-tuple-element.44), channel_id=1, source_target_pairs={{0,32},{8,40},{16,48},{24,56},{32,0},{40,8},{48,16},{56,24},{1,33}... | collective-permute-start | bytes 1769480 | tf_op jit(solution)/shard_map/ppermute | solution.py:136
  210.4 23.5 %collective-permute-start.1 = (bf16[384,768]{1,0:T(8,128)(2,1)}, bf16[384,768]{1,0:T(8,128)(2,1)}, u32[]{:S(2)}, u32[]{:S(2)}) collective-permute-start(bf16[384,768]{1,0:T(8,128)(2,1)} %get-tuple-element.45), channel_id=1, source_target_pairs={{0,32},{8,40},{16,48},{24,56},{32,0},{40,8},{48,16},{56,24},{1,33}... | collective-permute-start | bytes 1769480 | tf_op jit(solution)/shard_map/ppermute | solution.py:136
  216.8 17.1 %copy-start.12 = (bf16[384,768]{1,0:T(8,128)(2,1)S(1)}, bf16[384,768]{1,0:T(8,128)(2,1)}, u32[]{:S(2)}) copy-start(bf16[384,768]{1,0:T(8,128)(2,1)} %get-tuple-element.45) | copy-start | bytes 1769476
  216.8 29.3 %all-to-all-start.1 = ((bf16[8,48,2048]{2,1,0:T(8,128)(2,1)}), bf16[8,48,2048]{2,1,0:T(8,128)(2,1)S(1)}, u32[]{:S(2)}, u32[]{:S(2)}) async-start(bf16[8,48,2048]{2,1,0:T(8,128)(2,1)} %bitcast.88), calls=%async_computation.1 | async-start | bytes 3145728 | tf_op jit(solution)/shard_map/all_to_all | solution.py:95
  222.9 146.8 %reduce-scatter.6.cloned.1.call-start = ((), (), s32[]{:S(2)}) async-start(), calls=%async_computation.13 | async-start | bytes 3932160 | tf_op jit(solution)/shard_map/reduce_scatter | solution.py:141
  238.8 3.5 copy-start.11
  246.1 25.8 %all-to-all-start.4 = ((bf16[8,48,2048]{2,1,0:T(8,128)(2,1)}), bf16[8,48,2048]{2,1,0:T(8,128)(2,1)S(1)}, u32[]{:S(2)}, u32[]{:S(2)}) async-start(bf16[8,48,2048]{2,1,0:T(8,128)(2,1)} %bitcast.87), calls=%async_computation.4 | async-start | bytes 3145728 | tf_op jit(solution)/shard_map/all_to_all | solution.py:95
  251.3 2.0 copy-start.5
  271.8 60.0 %all-to-all-start.2 = ((bf16[8,32,2176]{2,1,0:T(8,128)(2,1)}), bf16[8,32,2176]{2,1,0:T(8,128)(2,1)S(1)}, u32[]{:S(2)}, u32[]{:S(2)}) async-start(bf16[8,32,2176]{2,1,0:T(8,128)(2,1)} %bitcast.12), calls=%async_computation.2 | async-start | bytes 2228224 | tf_op jit(solution)/shard_map/all_to_all | solution.py:100
  331.8 4.3 %copy-start.2 = (bf16[8,32,2176]{2,1,0:T(8,128)(2,1)}, bf16[8,32,2176]{2,1,0:T(8,128)(2,1)S(1)}, u32[]{:S(2)}) copy-start(bf16[8,32,2176]{2,1,0:T(8,128)(2,1)S(1)} %all-to-all-done.2) | copy-start | bytes 3342340
  331.8 33.5 %all-to-all-start.5 = ((bf16[8,32,2048]{2,1,0:T(8,128)(2,1)}), bf16[8,32,2048]{2,1,0:T(8,128)(2,1)}, u32[]{:S(2)}, u32[]{:S(2)}) async-start(bf16[8,32,2048]{2,1,0:T(8,128)(2,1)} %bitcast.92), calls=%async_computation.5 | async-start | bytes 2097152 | tf_op jit(solution)/shard_map/all_to_all | solution.py:100
  336.9 32.8 %copy-start.1 = (bf16[1,768,2048]{2,1,0:T(8,128)(2,1)S(1)}, bf16[1,768,2048]{2,1,0:T(8,128)(2,1)}, u32[]{:S(2)}) copy-start(bf16[1,768,2048]{2,1,0:T(8,128)(2,1)} %param.13) | copy-start | bytes 9437188
Sparse Core Ops, SparseCore 0:
  11.1 74.6 all-gather.1
  147.3 52.2 reduce-scatter.7
  210.5 62.4 reduce-scatter.3
  275.9 40.5 reduce-scatter.5
where the time goes:
time: 378 us; the launch traced here: 376 us
  waiting for transfers between devices  190 us (50%)
  starting transfers between devices  81.9 us (22%)
  matrix products  56 us (15%)
  local copies, waits for them, and re-layouts  22.3 us (6%)
  between operations  14.7 us (4%)
  other arithmetic  11.2 us (3%)
    all_to_all x1, waiting for transfers between devices, on_device(): lax.all_to_all(outbound, ('x', 'core', 'z'), split_axis=0, concat_axis=0,...  63.8 us
    dot_general x20, matrix products, dot(): lax.dot_general(left, right, (((lc,), (rc,)), ((), ())), preferred_elemen...  56 us
    all_to_all x2, waiting for transfers between devices, to_column(): return lax.all_to_all(rows, 'z', split_axis=0, concat_axis=0, tiled=True)  55 us
    all_to_all x5, waiting for transfers between devices, to_plane(): rows = lax.all_to_all(rows, PLANE, split_axis=0, concat_axis=0, tiled=True)  42.2 us
    all_to_all x2, starting transfers between devices, to_column(): return lax.all_to_all(rows, 'z', split_axis=0, concat_axis=0, tiled=True)  33.6 us
    ppermute x3, waiting for transfers between devices, placed(): other = lax.ppermute(own, 'z', [(i, i ^ N_Z // 2) for i in range(N_Z)])  29 us
    all_to_all x5, starting transfers between devices, to_plane(): rows = lax.all_to_all(rows, PLANE, split_axis=0, concat_axis=0, tiled=True)  26.6 us
    all_to_all x1, starting transfers between devices, on_device(): lax.all_to_all(outbound, ('x', 'core', 'z'), split_axis=0, concat_axis=0,...  13.3 us
  transfers between devices with their start and end apart: 15, of which 9 were waited for; matrix products, arithmetic and copies ran while one was open for 19% of the time, Pallas kernels for 0%

commit v1 on v0

--- a/solution.py
+++ b/solution.py
@@ -50,23 +50,6 @@
         + meta_col[:, 2 * top_count : 3 * top_count]
         + meta_col[:, 3 * top_count :]
     )
-
-    block = jnp.arange(experts, dtype=jnp.int32)
-    block_expert = block % N_Z * plane + block // N_Z
-    sent = jnp.any(routes[:, None, :] == block_expert[None, :, None], axis=2)
-    own_row = jnp.arange(tok_count, dtype=jnp.int32)
-    own_position = dot(
-        (own_row[:, None] > own_row[None, :]).astype(BF16), sent.astype(BF16)
-    ).astype(jnp.int32)
-    own_pick = jnp.where(sent, own_position, -1).T[:, None, :] == jnp.arange(
-        capacity, dtype=jnp.int32
-    )[None, :, None]
-    own_pick = own_pick.reshape(slots, tok_count).astype(BF16)
-    outbound = dot(own_pick, tokens).astype(BF16).reshape(experts, capacity, model_width)
-    rows_in = lax.all_to_all(
-        outbound, ("x", "core", "z"), split_axis=0, concat_axis=0, tiled=True
-    ).reshape(slots, model_width)
-
     row = jnp.arange(column, dtype=jnp.int32)
     earlier = (
         (row[:, None] > row[None, :])
@@ -74,7 +57,7 @@
     ).astype(BF16)
     slot_ids = jnp.arange(slots, dtype=jnp.int32).reshape(plane, per_expert)
 
-    def selection(ids):
+    def selection(ids, routes_col):
         named = routes_col[:, None, :] == ids[None, :, None]
         member = jnp.any(named, axis=2)
         gate_of = jnp.sum(jnp.where(named, gates_col[:, None, :], 0.0), axis=2)
@@ -108,14 +91,15 @@
         return to_plane(rows)
 
     plane_ids = z_index * plane + jnp.arange(plane, dtype=jnp.int32)
-    pick, slot_gate = selection(plane_ids)
+    pick, slot_gate = selection(plane_ids, routes_col)
+    rows_in = token_rows(pick)
     cot_rows = cot_pairs(pick, slot_gate)
 
     plane_flags = lax.dynamic_slice(swap_flags, (z_index * plane,), (plane,))
-    placed_pick, placed_gate = selection(
-        jnp.where(plane_flags == 1, plane_ids ^ (experts // 2), plane_ids)
+    later_routes, _ = lax.optimization_barrier((routes_col, rows_in))
+    placed_pick, _ = selection(
+        jnp.where(plane_flags == 1, plane_ids ^ (experts // 2), plane_ids), later_routes
     )
-    placed_cot = cot_pairs(placed_pick, placed_gate)
     placed_tok = token_rows(placed_pick)
 
     pre_gate = dot(rows_in, gate_mat)
@@ -130,7 +114,9 @@
     )
     grad_up_pre = (d_hidden * activated).astype(BF16)
     result = dot(hidden, down_mat).astype(BF16)
-    d_rows = (dot(grad_gate_pre, gate_mat, 1, 1) + dot(grad_up_pre, up_mat, 1, 1)).astype(BF16)
+    d_rows = (
+        dot(grad_gate_pre, gate_mat, 1, 1) + dot(grad_up_pre, up_mat, 1, 1)
+    ).astype(BF16)
 
     def placed(own):
         other = lax.ppermute(own, "z", [(i, i ^ (N_Z // 2)) for i in range(N_Z)])
@@ -140,7 +126,7 @@
         partial = dot(left, right, 0, 0).astype(BF16)
         return lax.psum_scatter(partial, "dp", scatter_dimension=0, tiled=True)
 
-    g_down = reduced(placed_cot, placed(hidden)).T[None]
+    g_down = placed(reduced(cot_rows, hidden)).T[None]
     g_gate = reduced(placed_tok, placed(grad_gate_pre))[None]
     g_up = reduced(placed_tok, placed(grad_up_pre))[None]
 

time: 378 us -> 366 us (0.968)
  the two profiles are of different devices: /device:TPU:1 before, /device:TPU:16 now
where the time goes in v1:
time: 366 us; the launch traced here: 365 us
  waiting for transfers between devices  218 us (60%)
  matrix products  59.6 us (16%)
  starting transfers between devices  42.3 us (12%)
  local copies, waits for them, and re-layouts  16.5 us (5%)
  between operations  14.7 us (4%)
  other arithmetic  13.1 us (4%)
    ppermute x3, waiting for transfers between devices, placed(): other = lax.ppermute(own, 'z', [(i, i ^ N_Z // 2) for i in range(N_Z)])  88.5 us
    dot_general x18, matrix products, dot(): lax.dot_general(left, right, (((lc,), (rc,)), ((), ())), preferred_elemen...  59.6 us
    all_to_all x5, waiting for transfers between devices, to_plane(): rows = lax.all_to_all(rows, PLANE, split_axis=0, concat_axis=0, tiled=True)  48.8 us
    all_gather x1, waiting for transfers between devices, on_device(): lax.all_gather(jnp.concatenate([tokens, d_out, meta], axis=1), 'z', tiled...  43 us
    all_to_all x2, waiting for transfers between devices, to_column(): return lax.all_to_all(rows, 'z', split_axis=0, concat_axis=0, tiled=True)  38.1 us
    all_to_all x5, starting transfers between devices, to_plane(): rows = lax.all_to_all(rows, PLANE, split_axis=0, concat_axis=0, tiled=True)  21.7 us
    ppermute x3, starting transfers between devices, placed(): other = lax.ppermute(own, 'z', [(i, i ^ N_Z // 2) for i in range(N_Z)])  11.9 us
    all_to_all x2, starting transfers between devices, to_column(): return lax.all_to_all(rows, 'z', split_axis=0, concat_axis=0, tiled=True)  8.5 us
  transfers between devices with their start and end apart: 14, of which 9 were waited for; matrix products, arithmetic and copies ran while one was open for 19% of the time, Pallas kernels for 0%

profile of v1, /device:TPU:16, one launch (start us, length us, event | category | flops | bytes accessed | tf_op | source)
XLA Modules:
  0.0 364.6 jit_solution(17383313575380883220)
XLA Ops:
  7.2 0.8 convert_element_type.107
  8.2 0.7 fusion.63
  9.1 1.8 concatenate.6
  11.0 0.7 compare_select_fusion.2
  11.8 43.0 %all-gather.2.cloned.1.call-done = bf16[256,4224]{1,0:T(8,128)(2,1)} async-done(((bf16[32,4224]{1,0:T(8,128)(2,1)}), bf16[256,4224]{1,0:T(8,128)(2,1)}) %all-gather.2.cloned.1.call-update) | async-done | bytes 2162704 | tf_op jit(solution)/shard_map/all_gather | solution.py:43
  54.7 0.8 slice_convert_fusion.1
  55.6 0.2 slice_add_fusion
  55.8 0.1 compare_reduce_fusion
  55.9 0.2 fusion.24
  56.2 0.8 eq.122
  57.0 1.9 copy.49
  58.9 1.0 broadcast_compare_fusion
  59.9 3.0 convolution_convert_fusion.4
  62.9 4.3 %all-to-all-start = ((bf16[8,48,2048]{2,1,0:T(8,128)(2,1)}), bf16[8,48,2048]{2,1,0:T(8,128)(2,1)}, u32[]{:S(2)}, u32[]{:S(2)}) async-start(bf16[8,48,2048]{2,1,0:T(8,128)(2,1)} %bitcast.81), calls=%async_computation | async-start | bytes 3145728 | tf_op jit(solution)/shard_map/all_to_all | solution.py:78
  67.4 0.2 fusion.35
  67.7 3.0 multiply_convert_fusion
  70.7 18.1 %all-to-all-done = bf16[8,48,2048]{2,1,0:T(8,128)(2,1)} async-done(((bf16[8,48,2048]{2,1,0:T(8,128)(2,1)}), bf16[8,48,2048]{2,1,0:T(8,128)(2,1)}, u32[]{:S(2)}, u32[]{:S(2)}) %all-to-all-start) | async-done | bytes 1572896 | tf_op jit(solution)/shard_map/all_to_all | solution.py:78
  88.9 4.3 %all-to-all-start.3 = ((bf16[8,48,2048]{2,1,0:T(8,128)(2,1)}), bf16[8,48,2048]{2,1,0:T(8,128)(2,1)}, u32[]{:S(2)}, u32[]{:S(2)}) async-start(bf16[8,48,2048]{2,1,0:T(8,128)(2,1)} %bitcast.84), calls=%async_computation.3 | async-start | bytes 3145728 | tf_op jit(solution)/shard_map/all_to_all | solution.py:78
  93.2 3.7 %fusion.10 = f32[384,768]{1,0:T(8,128)S(1)} fusion(bf16[384,2048]{1,0:T(8,128)(2,1)} %bitcast.4, bf16[1,2048,768]{2,1,0:T(8,128)(2,1)} %param.11), kind=kOutput, calls=%fused_computation.13 | convolution fusion | flops 1207959552 | bytes 5898240 | tf_op jit(solution)/shard_map/dot_general | solution.py:13
  97.0 1.1 copy-done.7
  98.1 4.0 %multiply_convert_fusion.3 = (bf16[384,768]{1,0:T(8,128)(2,1)}, f32[384,768]{1,0:T(8,128)}) fusion(f32[384,768]{1,0:T(8,128)S(1)} %fusion.10, bf16[384,2048]{1,0:T(8,128)(2,1)} %bitcast.4, bf16[1,2048,768]{2,1,0:T(8,128)(2,1)S(1)} %copy-done), kind=kOutput, calls=%fused_computation.30 | convolution fusion | flops 1209729024 | bytes 7667712 | tf_op jit(solution)/shard_map/dot_general | solution.py:13
  102.1 12.6 %all-to-all-done.3 = bf16[8,48,2048]{2,1,0:T(8,128)(2,1)} async-done(((bf16[8,48,2048]{2,1,0:T(8,128)(2,1)}), bf16[8,48,2048]{2,1,0:T(8,128)(2,1)}, u32[]{:S(2)}, u32[]{:S(2)}) %all-to-all-start.3) | async-done | bytes 1572896 | tf_op jit(solution)/shard_map/all_to_all | solution.py:78
  114.7 5.0 %convolution_convert_fusion = bf16[2048,768]{1,0:T(8,128)(2,1)} fusion(bf16[384,2048]{1,0:T(8,128)(2,1)} %bitcast.15, bf16[384,768]{1,0:T(8,128)(2,1)} %get-tuple-element.50), kind=kOutput, calls=%fused_computation | convolution fusion | flops 1209532416 | bytes 5308416 | tf_op jit(solution)/shard_map/dot_general | solution.py:13
  119.9 0.5 copy-done.6
  120.4 0.2 fusion.22
  120.6 0.8 eq.137
  121.4 1.9 copy.56
  123.3 3.1 convolution_convert_fusion.3
  126.5 4.3 %all-to-all-start.6 = ((bf16[8,48,2048]{2,1,0:T(8,128)(2,1)}), bf16[8,48,2048]{2,1,0:T(8,128)(2,1)}, u32[]{:S(2)}, u32[]{:S(2)}) async-start(bf16[8,48,2048]{2,1,0:T(8,128)(2,1)} %bitcast.80), calls=%async_computation.6 | async-start | bytes 3145728 | tf_op jit(solution)/shard_map/all_to_all | solution.py:78
  130.9 5.8 %multiply_convert_fusion.2 = (bf16[384,768]{1,0:T(8,128)(2,1)}, bf16[384,768]{1,0:T(8,128)(2,1)}) fusion(f32[384,768]{1,0:T(8,128)} %copy-done.7, f32[384,768]{1,0:T(8,128)} %get-tuple-element.51, bf16[384,2048]{1,0:T(8,128)(2,1)} %bitcast.15, bf16[1,768,2048]{2,1,0:T(8,128)(2,1)} %param.13), kind=kOutput, calls=%fused_computation.29 | convolution fusion | flops 1211793408 | bytes 8257536 | tf_op jit(solution)/shard_map/dot_general | solution.py:13
  136.6 3.3 collective-permute-start.1
  139.9 0.6 dynamic_slice.7
  141.1 27.9 %collective-permute-done.1 = bf16[384,768]{1,0:T(8,128)(2,1)} collective-permute-done((bf16[384,768]{1,0:T(8,128)(2,1)}, bf16[384,768]{1,0:T(8,128)(2,1)}, u32[]{:S(2)}, u32[]{:S(2)}) %collective-permute-start.1) | collective-permute-done | bytes 589856 | tf_op jit(solution)/shard_map/ppermute | solution.py:122
  169.0 5.1 %convolution_convert_fusion.1 = bf16[2048,768]{1,0:T(8,128)(2,1)} fusion(bf16[384,2048]{1,0:T(8,128)(2,1)} %bitcast.22, bf16[384,768]{1,0:T(8,128)(2,1)} %collective-permute-done.1, bf16[384,768]{1,0:T(8,128)(2,1)} %get-tuple-element.41, pred[]{:T(512)} %bitcast.23), kind=kOutput, calls=%fused_computation.1 | convolution fusion | flops 1209827328 | bytes 5898241 | tf_op jit(solution)/shard_map/dot_general | solution.py:13
  174.1 2.6 fusion.4
  176.8 2.6 add_convert_fusion
  179.3 4.3 %all-to-all-start.4 = ((bf16[8,48,2048]{2,1,0:T(8,128)(2,1)}), bf16[8,48,2048]{2,1,0:T(8,128)(2,1)}, u32[]{:S(2)}, u32[]{:S(2)}) async-start(bf16[8,48,2048]{2,1,0:T(8,128)(2,1)} %bitcast.83), calls=%async_computation.4 | async-start | bytes 3145728 | tf_op jit(solution)/shard_map/all_to_all | solution.py:78
  183.7 2.9 collective-permute-start
  186.6 29.8 %collective-permute-done = bf16[384,768]{1,0:T(8,128)(2,1)S(1)} collective-permute-done((bf16[384,768]{1,0:T(8,128)(2,1)}, bf16[384,768]{1,0:T(8,128)(2,1)S(1)}, u32[]{:S(2)}, u32[]{:S(2)}) %collective-permute-start) | collective-permute-done | bytes 589856 | tf_op jit(solution)/shard_map/ppermute | solution.py:122
  216.4 5.0 %convolution_convert_fusion.2 = bf16[2048,768]{1,0:T(8,128)(2,1)} fusion(bf16[384,2048]{1,0:T(8,128)(2,1)} %bitcast.22, bf16[384,768]{1,0:T(8,128)(2,1)S(1)} %collective-permute-done, bf16[384,768]{1,0:T(8,128)(2,1)} %get-tuple-element.40, pred[]{:T(512)} %bitcast.23), kind=kOutput, calls=%fused_computation.2 | convolution fusion | flops 1209827328 | bytes 5898241 | tf_op jit(solution)/shard_map/dot_general | solution.py:13
  221.4 4.6 %fusion.14 = bf16[384,2048]{1,0:T(8,128)(2,1)} fusion(bf16[384,768]{1,0:T(8,128)(2,1)} %get-tuple-element.50, bf16[1,768,2048]{2,1,0:T(8,128)(2,1)} %param.13), kind=kOutput, calls=%fused_computation.18 | convolution fusion | flops 1208745984 | bytes 5308416 | tf_op jit(solution)/shard_map/dot_general | solution.py:13
  226.0 4.4 %all-to-all-start.1 = ((bf16[8,48,2048]{2,1,0:T(8,128)(2,1)}), bf16[8,48,2048]{2,1,0:T(8,128)(2,1)}, u32[]{:S(2)}, u32[]{:S(2)}) async-start(bf16[8,48,2048]{2,1,0:T(8,128)(2,1)} %bitcast.85), calls=%async_computation.1 | async-start | bytes 3145728 | tf_op jit(solution)/shard_map/all_to_all | solution.py:78
  230.4 3.6 fusion.19
  234.0 18.1 %all-to-all-done.1 = bf16[8,48,2048]{2,1,0:T(8,128)(2,1)} async-done(((bf16[8,48,2048]{2,1,0:T(8,128)(2,1)}), bf16[8,48,2048]{2,1,0:T(8,128)(2,1)}, u32[]{:S(2)}, u32[]{:S(2)}) %all-to-all-start.1) | async-done | bytes 1572896 | tf_op jit(solution)/shard_map/all_to_all | solution.py:78
  252.1 4.2 %all-to-all-start.5 = ((bf16[8,32,2048]{2,1,0:T(8,128)(2,1)}), bf16[8,32,2048]{2,1,0:T(8,128)(2,1)}, u32[]{:S(2)}, u32[]{:S(2)}) async-start(bf16[8,32,2048]{2,1,0:T(8,128)(2,1)} %bitcast.88), calls=%async_computation.5 | async-start | bytes 2097152 | tf_op jit(solution)/shard_map/all_to_all | solution.py:83
  256.4 2.5 convolution_multiply_fusion
  258.9 0.9 select_reduce_fusion
  259.9 0.1 copy.54
  260.0 0.1 copy.53
  260.1 0.1 copy.52
  260.2 2.3 convolution_bitcast_fusion.1
  262.5 3.2 fusion.18
  265.8 3.1 concatenate.7
  268.9 16.2 %all-to-all-done.5 = bf16[8,32,2048]{2,1,0:T(8,128)(2,1)} async-done(((bf16[8,32,2048]{2,1,0:T(8,128)(2,1)}), bf16[8,32,2048]{2,1,0:T(8,128)(2,1)}, u32[]{:S(2)}, u32[]{:S(2)}) %all-to-all-start.5) | async-done | bytes 1048608 | tf_op jit(solution)/shard_map/all_to_all | solution.py:83
  285.0 4.3 %all-to-all-start.2 = ((bf16[8,32,2176]{2,1,0:T(8,128)(2,1)}), bf16[8,32,2176]{2,1,0:T(8,128)(2,1)}, u32[]{:S(2)}, u32[]{:S(2)}) async-start(bf16[8,32,2176]{2,1,0:T(8,128)(2,1)} %bitcast.82), calls=%async_computation.2 | async-start | bytes 2228224 | tf_op jit(solution)/shard_map/all_to_all | solution.py:83
  289.3 5.8 %collective-permute-start.2 = (bf16[512,768]{1,0:T(8,128)(2,1)}, bf16[512,768]{1,0:T(8,128)(2,1)}, u32[]{:S(2)}, u32[]{:S(2)}) collective-permute-start(bf16[512,768]{1,0:T(8,128)(2,1)} %reduce-scatter.8.cloned.1.call-done), channel_id=1, source_target_pairs={{0,32},{8,40},{16,48},{24,56},{32,0},{40,8},{48,16},{56,24},{1,33}... | collective-permute-start | bytes 2359304 | tf_op jit(solution)/shard_map/ppermute | solution.py:122
  295.1 2.1 reduce_sum.64
  297.2 21.9 %all-to-all-done.2 = bf16[8,32,2176]{2,1,0:T(8,128)(2,1)} async-done(((bf16[8,32,2176]{2,1,0:T(8,128)(2,1)}), bf16[8,32,2176]{2,1,0:T(8,128)(2,1)}, u32[]{:S(2)}, u32[]{:S(2)}) %all-to-all-start.2) | async-done | bytes 1114144 | tf_op jit(solution)/shard_map/all_to_all | solution.py:83
  319.1 0.9 convert_reduce_fusion
  320.0 0.7 copy.57
  320.7 2.1 slice_reduce_fusion
  322.8 30.8 %collective-permute-done.2 = bf16[512,768]{1,0:T(8,128)(2,1)} collective-permute-done((bf16[512,768]{1,0:T(8,128)(2,1)}, bf16[512,768]{1,0:T(8,128)(2,1)}, u32[]{:S(2)}, u32[]{:S(2)}) %collective-permute-start.2) | collective-permute-done | bytes 786464 | tf_op jit(solution)/shard_map/ppermute | solution.py:122
  353.7 2.1 select_bitcast_fusion
  355.8 2.3 copy.58
  (47 shorter events, 1.4 us)
Async XLA Ops:
  7.2 90.9 %copy-start = (bf16[1,2048,768]{2,1,0:T(8,128)(2,1)S(1)}, bf16[1,2048,768]{2,1,0:T(8,128)(2,1)}, u32[]{:S(2)}) copy-start(bf16[1,2048,768]{2,1,0:T(8,128)(2,1)} %param.12) | copy-start | bytes 9437188
  7.2 47.6 %all-gather.2.cloned.1.call-start = ((), (), s32[]{:S(2)}) async-start(), calls=%async_computation.10 | async-start | bytes 2433024 | tf_op jit(solution)/shard_map/all_gather | solution.py:43
  11.0 51.9 %copy-start.5 = (s32[8]{0:T(128)}, s32[8]{0:T(128)S(1)}, u32[]{:S(2)}) copy-start(s32[8]{0:T(128)S(1)} %iota_multiply_fusion) | copy-start | bytes 100
  62.9 25.9 %all-to-all-start = ((bf16[8,48,2048]{2,1,0:T(8,128)(2,1)}), bf16[8,48,2048]{2,1,0:T(8,128)(2,1)}, u32[]{:S(2)}, u32[]{:S(2)}) async-start(bf16[8,48,2048]{2,1,0:T(8,128)(2,1)} %bitcast.81), calls=%async_computation | async-start | bytes 3145728 | tf_op jit(solution)/shard_map/all_to_all | solution.py:78
  88.9 25.9 %all-to-all-start.3 = ((bf16[8,48,2048]{2,1,0:T(8,128)(2,1)}), bf16[8,48,2048]{2,1,0:T(8,128)(2,1)}, u32[]{:S(2)}, u32[]{:S(2)}) async-start(bf16[8,48,2048]{2,1,0:T(8,128)(2,1)} %bitcast.84), calls=%async_computation.3 | async-start | bytes 3145728 | tf_op jit(solution)/shard_map/all_to_all | solution.py:78
  93.2 196.2 %reduce-scatter.8.cloned.1.call-start = ((), (), s32[]{:S(2)}) async-start(), calls=%async_computation.13 | async-start | bytes 3932160 | tf_op jit(solution)/shard_map/reduce_scatter | solution.py:127
  97.0 1.1 copy-start.7
  119.7 0.7 copy-start.6
  126.5 42.6 %all-to-all-start.6 = ((bf16[8,48,2048]{2,1,0:T(8,128)(2,1)}), bf16[8,48,2048]{2,1,0:T(8,128)(2,1)}, u32[]{:S(2)}, u32[]{:S(2)}) async-start(bf16[8,48,2048]{2,1,0:T(8,128)(2,1)} %bitcast.80), calls=%async_computation.6 | async-start | bytes 3145728 | tf_op jit(solution)/shard_map/all_to_all | solution.py:78
  130.8 227.3 %reduce-scatter.6.cloned.1.call-start = ((), (), s32[]{:S(2)}) async-start(), calls=%async_computation.12 | async-start | bytes 3932160 | tf_op jit(solution)/shard_map/reduce_scatter | solution.py:127
  130.8 9.0 %copy-start.2 = (s32[64]{0:T(128)S(1)}, s32[64]{0:T(128)}, u32[]{:S(2)}) copy-start(s32[64]{0:T(128)} %param.14) | copy-start | bytes 772
  136.6 32.4 %collective-permute-start.1 = (bf16[384,768]{1,0:T(8,128)(2,1)}, bf16[384,768]{1,0:T(8,128)(2,1)}, u32[]{:S(2)}, u32[]{:S(2)}) collective-permute-start(bf16[384,768]{1,0:T(8,128)(2,1)} %get-tuple-element.41), channel_id=1, source_target_pairs={{0,32},{8,40},{16,48},{24,56},{32,0},{40,8},{48,16},{56,24},{1,33}... | collective-permute-start | bytes 1769480 | tf_op jit(solution)/shard_map/ppermute | solution.py:122
  174.1 2.7 copy-start.3
  174.1 2.7 copy-start.4
  179.3 46.7 %all-to-all-start.4 = ((bf16[8,48,2048]{2,1,0:T(8,128)(2,1)}), bf16[8,48,2048]{2,1,0:T(8,128)(2,1)}, u32[]{:S(2)}, u32[]{:S(2)}) async-start(bf16[8,48,2048]{2,1,0:T(8,128)(2,1)} %bitcast.83), calls=%async_computation.4 | async-start | bytes 3145728 | tf_op jit(solution)/shard_map/all_to_all | solution.py:78
  183.7 174.4 %reduce-scatter.4.cloned.1.call-start = ((), (), s32[]{:S(2)}) async-start(), calls=%async_computation.11 | async-start | bytes 3932160 | tf_op jit(solution)/shard_map/reduce_scatter | solution.py:127
  183.7 32.6 %collective-permute-start = (bf16[384,768]{1,0:T(8,128)(2,1)}, bf16[384,768]{1,0:T(8,128)(2,1)S(1)}, u32[]{:S(2)}, u32[]{:S(2)}) collective-permute-start(bf16[384,768]{1,0:T(8,128)(2,1)} %get-tuple-element.40), channel_id=1, source_target_pairs={{0,32},{8,40},{16,48},{24,56},{32,0},{40,8},{48,16},{56,24},{1,33}... | collective-permute-start | bytes 1769480 | tf_op jit(solution)/shard_map/ppermute | solution.py:122
  226.0 26.1 %all-to-all-start.1 = ((bf16[8,48,2048]{2,1,0:T(8,128)(2,1)}), bf16[8,48,2048]{2,1,0:T(8,128)(2,1)}, u32[]{:S(2)}, u32[]{:S(2)}) async-start(bf16[8,48,2048]{2,1,0:T(8,128)(2,1)} %bitcast.85), calls=%async_computation.1 | async-start | bytes 3145728 | tf_op jit(solution)/shard_map/all_to_all | solution.py:78
  252.1 33.0 %all-to-all-start.5 = ((bf16[8,32,2048]{2,1,0:T(8,128)(2,1)}), bf16[8,32,2048]{2,1,0:T(8,128)(2,1)}, u32[]{:S(2)}, u32[]{:S(2)}) async-start(bf16[8,32,2048]{2,1,0:T(8,128)(2,1)} %bitcast.88), calls=%async_computation.5 | async-start | bytes 2097152 | tf_op jit(solution)/shard_map/all_to_all | solution.py:83
  285.0 34.1 %all-to-all-start.2 = ((bf16[8,32,2176]{2,1,0:T(8,128)(2,1)}), bf16[8,32,2176]{2,1,0:T(8,128)(2,1)}, u32[]{:S(2)}, u32[]{:S(2)}) async-start(bf16[8,32,2176]{2,1,0:T(8,128)(2,1)} %bitcast.82), calls=%async_computation.2 | async-start | bytes 2228224 | tf_op jit(solution)/shard_map/all_to_all | solution.py:83
  289.3 64.4 %collective-permute-start.2 = (bf16[512,768]{1,0:T(8,128)(2,1)}, bf16[512,768]{1,0:T(8,128)(2,1)}, u32[]{:S(2)}, u32[]{:S(2)}) collective-permute-start(bf16[512,768]{1,0:T(8,128)(2,1)} %reduce-scatter.8.cloned.1.call-done), channel_id=1, source_target_pairs={{0,32},{8,40},{16,48},{24,56},{32,0},{40,8},{48,16},{56,24},{1,33}... | collective-permute-start | bytes 2359304 | tf_op jit(solution)/shard_map/ppermute | solution.py:122
  320.7 33.0 %copy-start.1 = (bf16[512,768]{1,0:T(8,128)(2,1)S(1)}, bf16[512,768]{1,0:T(8,128)(2,1)}, u32[]{:S(2)}) copy-start(bf16[512,768]{1,0:T(8,128)(2,1)} %reduce-scatter.8.cloned.1.call-done) | copy-start | bytes 2359300
Sparse Core Ops, SparseCore 0:
  11.0 43.6 all-gather.1
  119.9 36.2 reduce-scatter.7
  174.2 38.0 reduce-scatter.5
  221.5 37.8 reduce-scatter.3

commit v2 on v1

--- a/solution.py
+++ b/solution.py
@@ -45,33 +45,23 @@
     dout_col = gathered[:, model_width : 2 * model_width]
     meta_col = gathered[:, 2 * model_width : 2 * model_width + 4 * top_count].astype(F32)
     routes_col = meta_col[:, :top_count].astype(jnp.int32)
-    gates_col = (
-        meta_col[:, top_count : 2 * top_count]
-        + meta_col[:, 2 * top_count : 3 * top_count]
-        + meta_col[:, 3 * top_count :]
-    )
     row = jnp.arange(column, dtype=jnp.int32)
     earlier = (
         (row[:, None] > row[None, :])
         & (row[:, None] // tok_count == row[None, :] // tok_count)
     ).astype(BF16)
-    slot_ids = jnp.arange(slots, dtype=jnp.int32).reshape(plane, per_expert)
+    slot_ids = jnp.arange(slots, dtype=jnp.int32)
+    spread = (
+        slot_ids[:, None] // per_expert == jnp.arange(plane, dtype=jnp.int32)[None, :]
+    ).astype(BF16)
+    slot_rank = (slot_ids % per_expert).astype(F32)[:, None]
+    first_rank = (row // tok_count * capacity).astype(F32)[:, None]
 
     def selection(ids, routes_col):
         named = routes_col[:, None, :] == ids[None, :, None]
         member = jnp.any(named, axis=2)
-        gate_of = jnp.sum(jnp.where(named, gates_col[:, None, :], 0.0), axis=2)
-        position = dot(earlier, member.astype(BF16)).astype(jnp.int32)
-        slot_of = jnp.where(
-            member,
-            jnp.arange(plane, dtype=jnp.int32)[None, :] * per_expert
-            + (row // tok_count)[:, None] * capacity
-            + position,
-            -1,
-        )
-        pick = slot_of.T[:, None, :] == slot_ids[:, :, None]
-        slot_gate = jnp.sum(jnp.where(pick, gate_of.T[:, None, :], 0.0), axis=2)
-        return pick.astype(BF16).reshape(slots, column), slot_gate.reshape(slots, 1)
+        rank = jnp.where(member, first_rank + dot(earlier, member.astype(BF16)), -1.0)
+        return (dot(spread, rank.astype(BF16), 1, 1) == slot_rank).astype(BF16), named
 
     def to_plane(rows):
         rows = rows.reshape(plane, per_expert, -1)
@@ -91,8 +81,19 @@
         return to_plane(rows)
 
     plane_ids = z_index * plane + jnp.arange(plane, dtype=jnp.int32)
-    pick, slot_gate = selection(plane_ids, routes_col)
+    pick, named = selection(plane_ids, routes_col)
     rows_in = token_rows(pick)
+    gate_parts = [
+        jnp.sum(
+            jnp.where(named, meta_col[:, None, i * top_count : (i + 1) * top_count], 0.0), axis=2
+        ).astype(BF16)
+        for i in range(1, 4)
+    ]
+    slot_gate = jnp.sum(
+        dot(pick, jnp.concatenate(gate_parts, axis=1)) * jnp.tile(spread, (1, 3)).astype(F32),
+        axis=1,
+        keepdims=True,
+    )
     cot_rows = cot_pairs(pick, slot_gate)
 
     plane_flags = lax.dynamic_slice(swap_flags, (z_index * plane,), (plane,))
@@ -131,33 +132,32 @@
     g_up = reduced(placed_tok, placed(grad_up_pre))[None]
 
     out_rows = to_plane(result)
-    weight = jnp.where(
-        pick == 1, jnp.broadcast_to(slot_gate, pick.shape), 0.0
-    )
+    weight = jnp.where(pick == 1, jnp.broadcast_to(slot_gate, pick.shape), 0.0)
     weight_hi = lax.reduce_precision(weight, 8, 7)
     weight_lo = (weight - weight_hi).astype(BF16)
     mix_part = dot(weight_hi.astype(BF16), out_rows, 0, 0) + dot(weight_lo, out_rows, 0, 0)
-    cross = dot(dout_col, out_rows, 1, 1)
+    mix_part = mix_part.astype(BF16)
+    cross = dot(dout_col, out_rows, 1, 1) * pick.T.astype(F32)
     slot_expert = z_index * plane + jnp.arange(slots, dtype=jnp.int32) // per_expert
-    cross = cross * pick.T.astype(F32)
     dg_part = jnp.sum(
         jnp.where(routes_col[:, :, None] == slot_expert[None, None, :], cross[:, None, :], 0.0),
         axis=2,
     )
-    parts = to_column(
-        jnp.concatenate([mix_part.astype(BF16), padded(split3(dg_part), 128)], axis=1),
+    back_rows = to_plane(d_rows)
+    dtok_part = dot(pick, back_rows, 0, 0).astype(BF16)
+    parts = to_column(jnp.concatenate([mix_part, dtok_part, padded(split3(dg_part), 128)], axis=1))
+    mixture = jnp.sum(parts[:, :, :model_width].astype(F32), axis=0).astype(BF16)
+    d_tokens = jnp.sum(
+        parts[:, :, model_width : 2 * model_width].astype(F32), axis=0
+    ).astype(BF16)
+    dg_sum = jnp.sum(
+        parts[:, :, 2 * model_width : 2 * model_width + 3 * top_count].astype(F32), axis=0
     )
-    mixture = jnp.sum(parts[:, :, :model_width].astype(F32), axis=0).astype(BF16)
-    dg_sum = jnp.sum(parts[:, :, model_width : model_width + 3 * top_count].astype(F32), axis=0)
     d_gates = (
         dg_sum[:, :top_count]
         + dg_sum[:, top_count : 2 * top_count]
         + dg_sum[:, 2 * top_count :]
     )
-    back_rows = to_plane(d_rows)
-    d_tokens = jnp.sum(
-        to_column(dot(pick, back_rows, 0, 0).astype(BF16)).astype(F32), axis=0
-    ).astype(BF16)
     return (mixture, d_tokens, d_gates, g_gate, g_up, g_down)
 
 

time: 366 us -> 340 us (0.929)
  waiting for transfers between devices: 218 us -> 192 us
    ppermute x3, waiting for transfers between devices: 88.5 us -> 55.4 us  [placed(): other = lax.ppermute(own, 'z', [(i, i ^ N_Z // 2) for i in range(N_Z)])]
    all_to_all x2 -> x1, waiting for transfers between devices: 38.1 us -> 43.6 us  [to_column(): return lax.all_to_all(rows, 'z', split_axis=0, concat_axis=0, tiled=True)]
    eq x4 -> x0, local copies, waits for them, and re-layouts: 5.41 us -> none  [selection(): pick = slot_of.T[:, None, :] == slot_ids[:, :, None]]
    all_to_all x2 -> x1, starting transfers between devices: 8.5 us -> 9.38 us  [to_column(): return lax.all_to_all(rows, 'z', split_axis=0, concat_axis=0, tiled=True)]
    dot_general x18 -> x19, matrix products: 59.6 us -> 59.9 us  [dot(): lax.dot_general(left, right, (((lc,), (rc,)), ((), ())), preferred_elemen...]
  transfers between devices with their start and end apart: 14 -> 13, of which waited for: 9 -> 8; matrix products, arithmetic and copies ran while one was open for 19% -> 22% of each run, Pallas kernels for 0% -> 0%
where the time goes in v2:
time: 340 us; the launch traced here: 338 us
  waiting for transfers between devices  192 us (56%)
  matrix products  59.9 us (18%)
  starting transfers between devices  42.4 us (12%)
  local copies, waits for them, and re-layouts  16.5 us (5%)
  between operations  14.7 us (4%)
  other arithmetic  13.1 us (4%)
    dot_general x19, matrix products, dot(): lax.dot_general(left, right, (((lc,), (rc,)), ((), ())), preferred_elemen...  59.9 us
    ppermute x3, waiting for transfers between devices, placed(): other = lax.ppermute(own, 'z', [(i, i ^ N_Z // 2) for i in range(N_Z)])  55.4 us
    all_to_all x5, waiting for transfers between devices, to_plane(): rows = lax.all_to_all(rows, PLANE, split_axis=0, concat_axis=0, tiled=True)  50.1 us
    all_to_all x1, waiting for transfers between devices, to_column(): return lax.all_to_all(rows, 'z', split_axis=0, concat_axis=0, tiled=True)  43.6 us
    all_gather x1, waiting for transfers between devices, on_device(): lax.all_gather(jnp.concatenate([tokens, d_out, meta], axis=1), 'z', tiled...  42.5 us
    all_to_all x5, starting transfers between devices, to_plane(): rows = lax.all_to_all(rows, PLANE, split_axis=0, concat_axis=0, tiled=True)  21.5 us
    ppermute x3, starting transfers between devices, placed(): other = lax.ppermute(own, 'z', [(i, i ^ N_Z // 2) for i in range(N_Z)])  11.4 us
    all_to_all x1, starting transfers between devices, to_column(): return lax.all_to_all(rows, 'z', split_axis=0, concat_axis=0, tiled=True)  9.38 us
  transfers between devices with their start and end apart: 13, of which 8 were waited for; matrix products, arithmetic and copies ran while one was open for 22% of the time, Pallas kernels for 0%

profile of v2, /device:TPU:16, one launch (start us, length us, event | category | flops | bytes accessed | tf_op | source)
XLA Modules:
  0.0 338.3 jit_solution(1002563239432648439)
XLA Ops:
  7.2 0.8 convert_element_type.143
  8.1 0.1 copy.39
  8.2 0.7 fusion.66
  8.9 0.1 copy.42
  8.9 0.1 copy.41
  9.1 1.8 concatenate.9
  10.9 1.2 compare_select_fusion.3
  12.2 42.5 %all-gather.2.cloned.1.call-done = bf16[256,4224]{1,0:T(8,128)(2,1)} async-done(((bf16[32,4224]{1,0:T(8,128)(2,1)}), bf16[256,4224]{1,0:T(8,128)(2,1)}) %all-gather.2.cloned.1.call-update) | async-done | bytes 2162704 | tf_op jit(solution)/shard_map/all_gather | solution.py:43
  54.7 0.8 slice_convert_fusion.1
  55.6 0.9 fusion.83
  56.5 0.1 compare_reduce_fusion
  56.6 0.5 convolution_compare_fusion.1
  57.1 3.0 convolution_convert_fusion.4
  60.1 4.3 %all-to-all-start = ((bf16[8,48,2048]{2,1,0:T(8,128)(2,1)}), bf16[8,48,2048]{2,1,0:T(8,128)(2,1)}, u32[]{:S(2)}, u32[]{:S(2)}) async-start(bf16[8,48,2048]{2,1,0:T(8,128)(2,1)} %bitcast.68), calls=%async_computation | async-start | bytes 3145728 | tf_op jit(solution)/shard_map/all_to_all | solution.py:68
  64.4 1.0 copy.45
  65.4 1.0 copy.46
  66.4 0.8 fusion.52
  67.2 0.2 fusion.19
  67.4 3.0 multiply_convert_fusion
  70.4 15.6 %all-to-all-done = bf16[8,48,2048]{2,1,0:T(8,128)(2,1)} async-done(((bf16[8,48,2048]{2,1,0:T(8,128)(2,1)}), bf16[8,48,2048]{2,1,0:T(8,128)(2,1)}, u32[]{:S(2)}, u32[]{:S(2)}) %all-to-all-start) | async-done | bytes 1572896 | tf_op jit(solution)/shard_map/all_to_all | solution.py:68
  86.0 4.3 %all-to-all-start.2 = ((bf16[8,48,2048]{2,1,0:T(8,128)(2,1)}), bf16[8,48,2048]{2,1,0:T(8,128)(2,1)}, u32[]{:S(2)}, u32[]{:S(2)}) async-start(bf16[8,48,2048]{2,1,0:T(8,128)(2,1)} %bitcast.70), calls=%async_computation.2 | async-start | bytes 3145728 | tf_op jit(solution)/shard_map/all_to_all | solution.py:68
  90.4 3.9 %fusion.10 = f32[384,768]{1,0:T(8,128)S(1)} fusion(bf16[384,2048]{1,0:T(8,128)(2,1)} %bitcast.2, bf16[1,2048,768]{2,1,0:T(8,128)(2,1)} %param.11), kind=kOutput, calls=%fused_computation.13 | convolution fusion | flops 1207959552 | bytes 5898240 | tf_op jit(solution)/shard_map/dot_general | solution.py:13
  94.3 1.1 copy-done.14
  95.4 4.0 %multiply_convert_fusion.3 = (bf16[384,768]{1,0:T(8,128)(2,1)}, f32[384,768]{1,0:T(8,128)}) fusion(f32[384,768]{1,0:T(8,128)S(1)} %fusion.10, bf16[384,2048]{1,0:T(8,128)(2,1)} %bitcast.2, bf16[1,2048,768]{2,1,0:T(8,128)(2,1)S(1)} %copy-done.11), kind=kOutput, calls=%fused_computation.27 | convolution fusion | flops 1209729024 | bytes 7667712 | tf_op jit(solution)/shard_map/dot_general | solution.py:13
  99.4 12.4 %all-to-all-done.2 = bf16[8,48,2048]{2,1,0:T(8,128)(2,1)} async-done(((bf16[8,48,2048]{2,1,0:T(8,128)(2,1)}), bf16[8,48,2048]{2,1,0:T(8,128)(2,1)}, u32[]{:S(2)}, u32[]{:S(2)}) %all-to-all-start.2) | async-done | bytes 1572896 | tf_op jit(solution)/shard_map/all_to_all | solution.py:68
  111.9 5.0 %convolution_convert_fusion = bf16[2048,768]{1,0:T(8,128)(2,1)} fusion(bf16[384,2048]{1,0:T(8,128)(2,1)} %bitcast.9, bf16[384,768]{1,0:T(8,128)(2,1)} %get-tuple-element.51), kind=kOutput, calls=%fused_computation | convolution fusion | flops 1209532416 | bytes 5308416 | tf_op jit(solution)/shard_map/dot_general | solution.py:13
  117.0 0.5 copy-done.5
  117.5 0.1 compare_reduce_fusion.1
  117.6 0.2 fusion.23
  117.8 3.1 convolution_convert_fusion.3
  121.0 4.3 %all-to-all-start.5 = ((bf16[8,48,2048]{2,1,0:T(8,128)(2,1)}), bf16[8,48,2048]{2,1,0:T(8,128)(2,1)}, u32[]{:S(2)}, u32[]{:S(2)}) async-start(bf16[8,48,2048]{2,1,0:T(8,128)(2,1)} %bitcast.67), calls=%async_computation.5 | async-start | bytes 3145728 | tf_op jit(solution)/shard_map/all_to_all | solution.py:68
  125.3 5.0 %multiply_convert_fusion.2 = (bf16[384,768]{1,0:T(8,128)(2,1)}, bf16[384,768]{1,0:T(8,128)(2,1)}) fusion(f32[384,768]{1,0:T(8,128)} %copy-done.14, f32[384,768]{1,0:T(8,128)} %get-tuple-element.52, bf16[384,2048]{1,0:T(8,128)(2,1)} %bitcast.9, bf16[1,768,2048]{2,1,0:T(8,128)(2,1)S(1)} %copy-done), kind=kOutput, calls=%fused_computation.26 | convolution fusion | flops 1211793408 | bytes 8257536 | tf_op jit(solution)/shard_map/dot_general | solution.py:13
  130.3 3.0 collective-permute-start.1
  133.3 0.6 dynamic_slice.7
  134.6 23.1 %collective-permute-done.1 = bf16[384,768]{1,0:T(8,128)(2,1)} collective-permute-done((bf16[384,768]{1,0:T(8,128)(2,1)}, bf16[384,768]{1,0:T(8,128)(2,1)}, u32[]{:S(2)}, u32[]{:S(2)}) %collective-permute-start.1) | collective-permute-done | bytes 589856 | tf_op jit(solution)/shard_map/ppermute | solution.py:123
  157.7 5.0 %convolution_convert_fusion.1 = bf16[2048,768]{1,0:T(8,128)(2,1)} fusion(bf16[384,2048]{1,0:T(8,128)(2,1)} %bitcast.15, bf16[384,768]{1,0:T(8,128)(2,1)} %collective-permute-done.1, bf16[384,768]{1,0:T(8,128)(2,1)} %get-tuple-element.40, pred[]{:T(512)} %bitcast.16), kind=kOutput, calls=%fused_computation.1 | convolution fusion | flops 1209827328 | bytes 5898241 | tf_op jit(solution)/shard_map/dot_general | solution.py:13
  162.8 3.6 %fusion.14 = bf16[384,2048]{1,0:T(8,128)(2,1)} fusion(bf16[384,768]{1,0:T(8,128)(2,1)} %get-tuple-element.51, bf16[1,768,2048]{2,1,0:T(8,128)(2,1)S(1)} %copy-done), kind=kOutput, calls=%fused_computation.18 | convolution fusion | flops 1208745984 | bytes 5308416 | tf_op jit(solution)/shard_map/dot_general | solution.py:13
  166.4 4.3 %all-to-all-start.1 = ((bf16[8,48,2048]{2,1,0:T(8,128)(2,1)}), bf16[8,48,2048]{2,1,0:T(8,128)(2,1)}, u32[]{:S(2)}, u32[]{:S(2)}) async-start(bf16[8,48,2048]{2,1,0:T(8,128)(2,1)} %bitcast.71), calls=%async_computation.1 | async-start | bytes 3145728 | tf_op jit(solution)/shard_map/all_to_all | solution.py:68
  170.8 2.5 collective-permute-start
  173.2 3.5 %fusion.4 = f32[384,2048]{1,0:T(8,128)S(1)} fusion(bf16[384,768]{1,0:T(8,128)(2,1)} %get-tuple-element.40, bf16[1,2048,768]{2,1,0:T(8,128)(2,1)} %param.12), kind=kOutput, calls=%fused_computation.7 | convolution fusion | flops 1207959552 | bytes 6881280 | tf_op jit(solution)/shard_map/dot_general | solution.py:13
  176.7 2.6 add_convert_fusion
  179.3 13.0 %all-to-all-done.1 = bf16[8,48,2048]{2,1,0:T(8,128)(2,1)} async-done(((bf16[8,48,2048]{2,1,0:T(8,128)(2,1)}), bf16[8,48,2048]{2,1,0:T(8,128)(2,1)}, u32[]{:S(2)}, u32[]{:S(2)}) %all-to-all-start.1) | async-done | bytes 1572896 | tf_op jit(solution)/shard_map/all_to_all | solution.py:68
  192.3 4.3 %all-to-all-start.3 = ((bf16[8,48,2048]{2,1,0:T(8,128)(2,1)}), bf16[8,48,2048]{2,1,0:T(8,128)(2,1)}, u32[]{:S(2)}, u32[]{:S(2)}) async-start(bf16[8,48,2048]{2,1,0:T(8,128)(2,1)} %bitcast.69), calls=%async_computation.3 | async-start | bytes 3145728 | tf_op jit(solution)/shard_map/all_to_all | solution.py:68
  196.7 5.1 %convolution_convert_fusion.2 = bf16[2048,768]{1,0:T(8,128)(2,1)} fusion(bf16[384,2048]{1,0:T(8,128)(2,1)} %bitcast.15, bf16[384,768]{1,0:T(8,128)(2,1)} %collective-permute-done, bf16[384,768]{1,0:T(8,128)(2,1)} %get-tuple-element.39, pred[]{:T(512)} %bitcast.16), kind=kOutput, calls=%fused_computation.2 | convolution fusion | flops 1209827328 | bytes 5898241 | tf_op jit(solution)/shard_map/dot_general | solution.py:13
  201.8 3.1 convolution_multiply_fusion
  204.9 1.9 copy.48
  206.8 1.8 select_reduce_fusion
  208.7 0.1 copy.53
  208.8 0.1 copy.52
  209.0 0.1 copy.51
  209.1 9.1 %all-to-all-done.3 = bf16[8,48,2048]{2,1,0:T(8,128)(2,1)} async-done(((bf16[8,48,2048]{2,1,0:T(8,128)(2,1)}), bf16[8,48,2048]{2,1,0:T(8,128)(2,1)}, u32[]{:S(2)}, u32[]{:S(2)}) %all-to-all-start.3) | async-done | bytes 1572896 | tf_op jit(solution)/shard_map/all_to_all | solution.py:68
  218.1 3.2 convolution_convert_fusion.5
  221.3 2.6 fusion.38
  223.9 3.3 fusion.17
  227.2 4.7 %concatenate.11 = bf16[256,4224]{1,0:T(8,128)(2,1)} concatenate(bf16[256,2048]{1,0:T(8,128)(2,1)} %fusion.17, bf16[256,2048]{1,0:T(8,128)(2,1)} %convolution_convert_fusion.5, bf16[256,8]{1,0:T(8,128)(2,1)S(1)} %copy.51, bf16[256,8]{1,0:T(8,128)(2,1)S(1)} %copy.52, bf16[256,8]{1,0:T(8,128)(2,1)S(1)} %copy.53, bf16[256,104]{1,0:T(8,128)(2,1)S(1)} %broadcast_in_dim.94), dimensions={1} | concatenate | bytes 4325376 | tf_op jit(solution)/shard_map/concatenate | solution.py:148
  231.8 9.4 %all-to-all-start.4 = ((bf16[8,32,4224]{2,1,0:T(8,128)(2,1)}), bf16[8,32,4224]{2,1,0:T(8,128)(2,1)}, u32[]{:S(2)}, u32[]{:S(2)}) async-start(bf16[8,32,4224]{2,1,0:T(8,128)(2,1)} %bitcast.66), calls=%async_computation.4 | async-start | bytes 4325376 | tf_op jit(solution)/shard_map/all_to_all | solution.py:73
  241.2 5.9 %collective-permute-start.2 = (bf16[512,768]{1,0:T(8,128)(2,1)}, bf16[512,768]{1,0:T(8,128)(2,1)}, u32[]{:S(2)}, u32[]{:S(2)}) collective-permute-start(bf16[512,768]{1,0:T(8,128)(2,1)} %reduce-scatter.8.cloned.1.call-done), channel_id=1, source_target_pairs={{0,32},{8,40},{16,48},{24,56},{32,0},{40,8},{48,16},{56,24},{1,33}... | collective-permute-start | bytes 2359304 | tf_op jit(solution)/shard_map/ppermute | solution.py:123
  247.2 43.6 %all-to-all-done.4 = bf16[8,32,4224]{2,1,0:T(8,128)(2,1)} async-done(((bf16[8,32,4224]{2,1,0:T(8,128)(2,1)}), bf16[8,32,4224]{2,1,0:T(8,128)(2,1)}, u32[]{:S(2)}, u32[]{:S(2)}) %all-to-all-start.4) | async-done | bytes 2162720 | tf_op jit(solution)/shard_map/all_to_all | solution.py:73
  290.7 0.9 convert_reduce_fusion
  291.7 0.7 copy.55
  292.4 2.7 slice_reduce_fusion
  295.1 32.3 %collective-permute-done.2 = bf16[512,768]{1,0:T(8,128)(2,1)} collective-permute-done((bf16[512,768]{1,0:T(8,128)(2,1)}, bf16[512,768]{1,0:T(8,128)(2,1)}, u32[]{:S(2)}, u32[]{:S(2)}) %collective-permute-start.2) | collective-permute-done | bytes 786464 | tf_op jit(solution)/shard_map/ppermute | solution.py:123
  327.4 2.1 select_bitcast_fusion
  329.5 2.3 copy.56
  (54 shorter events, 0.8 us)
Async XLA Ops:
  7.2 118.1 %copy-start = (bf16[1,768,2048]{2,1,0:T(8,128)(2,1)S(1)}, bf16[1,768,2048]{2,1,0:T(8,128)(2,1)}, u32[]{:S(2)}) copy-start(bf16[1,768,2048]{2,1,0:T(8,128)(2,1)} %param.13) | copy-start | bytes 9437188
  7.2 47.5 %all-gather.2.cloned.1.call-start = ((), (), s32[]{:S(2)}) async-start(), calls=%async_computation.9 | async-start | bytes 2433024 | tf_op jit(solution)/shard_map/all_gather | solution.py:43
  12.1 47.9 %copy-start.4 = (s32[8]{0:T(128)}, s32[8]{0:T(128)S(1)}, u32[]{:S(2)}) copy-start(s32[8]{0:T(128)S(1)} %get-tuple-element.54) | copy-start | bytes 100
  12.1 47.9 %copy-start.6 = (s32[256]{0:T(256)}, s32[256]{0:T(256)S(1)}, u32[]{:S(2)}) copy-start(s32[256]{0:T(256)S(1)} %get-tuple-element.57) | copy-start | bytes 3076
  12.2 47.9 %copy-start.8 = (f32[256]{0:T(256)}, f32[256]{0:T(256)S(1)}, u32[]{:S(2)}) copy-start(f32[256]{0:T(256)S(1)} %get-tuple-element.58) | copy-start | bytes 3076
  12.2 47.9 %copy-start.2 = (f32[384]{0:T(512)}, f32[384]{0:T(512)S(1)}, u32[]{:S(2)}) copy-start(f32[384]{0:T(512)S(1)} %get-tuple-element.56) | copy-start | bytes 4612
  60.1 25.9 %all-to-all-start = ((bf16[8,48,2048]{2,1,0:T(8,128)(2,1)}), bf16[8,48,2048]{2,1,0:T(8,128)(2,1)}, u32[]{:S(2)}, u32[]{:S(2)}) async-start(bf16[8,48,2048]{2,1,0:T(8,128)(2,1)} %bitcast.68), calls=%async_computation | async-start | bytes 3145728 | tf_op jit(solution)/shard_map/all_to_all | solution.py:68
  86.0 25.9 %all-to-all-start.2 = ((bf16[8,48,2048]{2,1,0:T(8,128)(2,1)}), bf16[8,48,2048]{2,1,0:T(8,128)(2,1)}, u32[]{:S(2)}, u32[]{:S(2)}) async-start(bf16[8,48,2048]{2,1,0:T(8,128)(2,1)} %bitcast.70), calls=%async_computation.2 | async-start | bytes 3145728 | tf_op jit(solution)/shard_map/all_to_all | solution.py:68
  90.3 150.9 %reduce-scatter.8.cloned.1.call-start = ((), (), s32[]{:S(2)}) async-start(), calls=%async_computation.12 | async-start | bytes 3932160 | tf_op jit(solution)/shard_map/reduce_scatter | solution.py:128
  90.4 5.0 %copy-start.11 = (bf16[1,2048,768]{2,1,0:T(8,128)(2,1)S(1)}, bf16[1,2048,768]{2,1,0:T(8,128)(2,1)}, u32[]{:S(2)}) copy-start(bf16[1,2048,768]{2,1,0:T(8,128)(2,1)} %param.12) | copy-start | bytes 9437188
  94.3 1.1 copy-start.14
  116.9 0.6 copy-start.5
  116.9 0.7 copy-start.7
  116.9 0.7 copy-start.9
  116.9 0.9 copy-start.3
  121.0 36.8 %all-to-all-start.5 = ((bf16[8,48,2048]{2,1,0:T(8,128)(2,1)}), bf16[8,48,2048]{2,1,0:T(8,128)(2,1)}, u32[]{:S(2)}, u32[]{:S(2)}) async-start(bf16[8,48,2048]{2,1,0:T(8,128)(2,1)} %bitcast.67), calls=%async_computation.5 | async-start | bytes 3145728 | tf_op jit(solution)/shard_map/all_to_all | solution.py:68
  125.3 206.5 %reduce-scatter.6.cloned.1.call-start = ((), (), s32[]{:S(2)}) async-start(), calls=%async_computation.11 | async-start | bytes 3932160 | tf_op jit(solution)/shard_map/reduce_scatter | solution.py:128
  125.3 8.0 %copy-start.10 = (s32[64]{0:T(128)S(1)}, s32[64]{0:T(128)}, u32[]{:S(2)}) copy-start(s32[64]{0:T(128)} %param.14) | copy-start | bytes 772
  130.3 27.4 %collective-permute-start.1 = (bf16[384,768]{1,0:T(8,128)(2,1)}, bf16[384,768]{1,0:T(8,128)(2,1)}, u32[]{:S(2)}, u32[]{:S(2)}) collective-permute-start(bf16[384,768]{1,0:T(8,128)(2,1)} %get-tuple-element.40), channel_id=1, source_target_pairs={{0,32},{8,40},{16,48},{24,56},{32,0},{40,8},{48,16},{56,24},{1,33}... | collective-permute-start | bytes 1769480 | tf_op jit(solution)/shard_map/ppermute | solution.py:123
  166.4 25.9 %all-to-all-start.1 = ((bf16[8,48,2048]{2,1,0:T(8,128)(2,1)}), bf16[8,48,2048]{2,1,0:T(8,128)(2,1)}, u32[]{:S(2)}, u32[]{:S(2)}) async-start(bf16[8,48,2048]{2,1,0:T(8,128)(2,1)} %bitcast.71), calls=%async_computation.1 | async-start | bytes 3145728 | tf_op jit(solution)/shard_map/all_to_all | solution.py:68
  170.7 6.0 %copy-start.12 = (bf16[1,2048,768]{2,1,0:T(8,128)(2,1)S(1)}, bf16[1,2048,768]{2,1,0:T(8,128)(2,1)}, u32[]{:S(2)}) copy-start(bf16[1,2048,768]{2,1,0:T(8,128)(2,1)} %param.11) | copy-start | bytes 9437188
  170.7 6.0 %copy-start.13 = (bf16[384,768]{1,0:T(8,128)(2,1)S(1)}, bf16[384,768]{1,0:T(8,128)(2,1)}, u32[]{:S(2)}) copy-start(bf16[384,768]{1,0:T(8,128)(2,1)} %get-tuple-element.39) | copy-start | bytes 1769476
  170.8 25.9 %collective-permute-start = (bf16[384,768]{1,0:T(8,128)(2,1)}, bf16[384,768]{1,0:T(8,128)(2,1)}, u32[]{:S(2)}, u32[]{:S(2)}) collective-permute-start(bf16[384,768]{1,0:T(8,128)(2,1)} %get-tuple-element.39), channel_id=1, source_target_pairs={{0,32},{8,40},{16,48},{24,56},{32,0},{40,8},{48,16},{56,24},{1,33}... | collective-permute-start | bytes 1769480 | tf_op jit(solution)/shard_map/ppermute | solution.py:123
  192.3 25.9 %all-to-all-start.3 = ((bf16[8,48,2048]{2,1,0:T(8,128)(2,1)}), bf16[8,48,2048]{2,1,0:T(8,128)(2,1)}, u32[]{:S(2)}, u32[]{:S(2)}) async-start(bf16[8,48,2048]{2,1,0:T(8,128)(2,1)} %bitcast.69), calls=%async_computation.3 | async-start | bytes 3145728 | tf_op jit(solution)/shard_map/all_to_all | solution.py:68
  196.6 135.2 %reduce-scatter.4.cloned.1.call-start = ((), (), s32[]{:S(2)}) async-start(), calls=%async_computation.10 | async-start | bytes 3932160 | tf_op jit(solution)/shard_map/reduce_scatter | solution.py:128
  231.8 58.9 %all-to-all-start.4 = ((bf16[8,32,4224]{2,1,0:T(8,128)(2,1)}), bf16[8,32,4224]{2,1,0:T(8,128)(2,1)}, u32[]{:S(2)}, u32[]{:S(2)}) async-start(bf16[8,32,4224]{2,1,0:T(8,128)(2,1)} %bitcast.66), calls=%async_computation.4 | async-start | bytes 4325376 | tf_op jit(solution)/shard_map/all_to_all | solution.py:73
  241.2 86.1 %collective-permute-start.2 = (bf16[512,768]{1,0:T(8,128)(2,1)}, bf16[512,768]{1,0:T(8,128)(2,1)}, u32[]{:S(2)}, u32[]{:S(2)}) collective-permute-start(bf16[512,768]{1,0:T(8,128)(2,1)} %reduce-scatter.8.cloned.1.call-done), channel_id=1, source_target_pairs={{0,32},{8,40},{16,48},{24,56},{32,0},{40,8},{48,16},{56,24},{1,33}... | collective-permute-start | bytes 2359304 | tf_op jit(solution)/shard_map/ppermute | solution.py:123
  292.4 35.0 %copy-start.1 = (bf16[512,768]{1,0:T(8,128)(2,1)S(1)}, bf16[512,768]{1,0:T(8,128)(2,1)}, u32[]{:S(2)}) copy-start(bf16[512,768]{1,0:T(8,128)(2,1)} %reduce-scatter.8.cloned.1.call-done) | copy-start | bytes 2359300
Sparse Core Ops, SparseCore 0:
  11.0 43.6 all-gather.1
  117.0 36.2 reduce-scatter.7
  162.9 43.1 reduce-scatter.5
  209.1 40.5 reduce-scatter.3

commit v3 on v2

--- a/solution.py
+++ b/solution.py
@@ -109,6 +109,8 @@
     activated = pre_gate * logistic
     hidden = (activated * pre_up).astype(BF16)
     _, cot_rows = lax.optimization_barrier((hidden, cot_rows))
+    down_partial = dot(cot_rows, hidden, 0, 0).astype(BF16)
+    down_partial, cot_rows = lax.optimization_barrier((down_partial, cot_rows))
     d_hidden = dot(cot_rows, down_mat, 1, 1)
     grad_gate_pre = (d_hidden * pre_up * logistic * (1.0 + pre_gate * (1.0 - logistic))).astype(
         BF16
@@ -123,13 +125,16 @@
         other = lax.ppermute(own, "z", [(i, i ^ (N_Z // 2)) for i in range(N_Z)])
         return jnp.where(own_flag == 1, other, own)
 
-    def reduced(left, right):
-        partial = dot(left, right, 0, 0).astype(BF16)
+    def reduced(partial):
         return lax.psum_scatter(partial, "dp", scatter_dimension=0, tiled=True)
 
-    g_down = placed(reduced(cot_rows, hidden)).T[None]
-    g_gate = reduced(placed_tok, placed(grad_gate_pre))[None]
-    g_up = reduced(placed_tok, placed(grad_up_pre))[None]
+    g_down = placed(reduced(down_partial)).T[None]
+    placed_gate_pre = placed(grad_gate_pre)
+    gate_partial = dot(placed_tok, placed_gate_pre, 0, 0).astype(BF16)
+    g_gate = reduced(gate_partial)[None]
+    placed_up_pre = placed(grad_up_pre)
+    up_partial = dot(placed_tok, placed_up_pre, 0, 0).astype(BF16)
+    g_up = reduced(up_partial)[None]
 
     out_rows = to_plane(result)
     weight = jnp.where(pick == 1, jnp.broadcast_to(slot_gate, pick.shape), 0.0)
@@ -140,24 +145,30 @@
     cross = dot(dout_col, out_rows, 1, 1) * pick.T.astype(F32)
     slot_expert = z_index * plane + jnp.arange(slots, dtype=jnp.int32) // per_expert
     dg_part = jnp.sum(
-        jnp.where(routes_col[:, :, None] == slot_expert[None, None, :], cross[:, None, :], 0.0),
+        jnp.where(
+            routes_col[:, :, None] == slot_expert[None, None, :], cross[:, None, :], 0.0
+        ),
         axis=2,
     )
-    back_rows = to_plane(d_rows)
-    dtok_part = dot(pick, back_rows, 0, 0).astype(BF16)
-    parts = to_column(jnp.concatenate([mix_part, dtok_part, padded(split3(dg_part), 128)], axis=1))
-    mixture = jnp.sum(parts[:, :, :model_width].astype(F32), axis=0).astype(BF16)
-    d_tokens = jnp.sum(
-        parts[:, :, model_width : 2 * model_width].astype(F32), axis=0
-    ).astype(BF16)
-    dg_sum = jnp.sum(
-        parts[:, :, 2 * model_width : 2 * model_width + 3 * top_count].astype(F32), axis=0
-    )
+    packed = jnp.concatenate([mix_part, padded(split3(dg_part), 128)], axis=1)
+
+    def summed(parts, first, width):
+        planes = [parts[i, :, first : first + width].astype(F32) for i in range(N_Z)]
+        while len(planes) > 1:
+            planes = [x + y for x, y in zip(planes[::2], planes[1::2])]
+        return planes[0]
+
+    mix_parts = to_column(packed)
+    mixture = summed(mix_parts, 0, model_width).astype(BF16)
+    dg_sum = summed(mix_parts, model_width, 3 * top_count)
     d_gates = (
         dg_sum[:, :top_count]
         + dg_sum[:, top_count : 2 * top_count]
         + dg_sum[:, 2 * top_count :]
     )
+    back_rows = to_plane(d_rows)
+    dtok_part = dot(pick, back_rows, 0, 0).astype(BF16)
+    d_tokens = summed(to_column(dtok_part), 0, model_width).astype(BF16)
     return (mixture, d_tokens, d_gates, g_gate, g_up, g_down)
 
 

time: 340 us -> 340 us (level)
  waiting for transfers between devices: 192 us -> 185 us
  starting transfers between devices: 42.4 us -> 49.1 us
    all_to_all x1 -> x2, waiting for transfers between devices: 43.6 us -> 34.5 us  [to_column(): return lax.all_to_all(rows, 'z', split_axis=0, concat_axis=0, tiled=True)]
    all_to_all x5, waiting for transfers between devices: 50.1 us -> 55.4 us  [to_plane(): rows = lax.all_to_all(rows, PLANE, split_axis=0, concat_axis=0, tiled=True)]
    add x0 -> x3, other arithmetic: none -> 5.05 us  [summed(): planes = [x + y for x, y in zip(planes[::2], planes[1::2])]]
    all_to_all x1 -> x2, starting transfers between devices: 9.38 us -> 13.4 us  [to_column(): return lax.all_to_all(rows, 'z', split_axis=0, concat_axis=0, tiled=True)]
    reduce_sum x2 -> x0, other arithmetic: 3.61 us -> none  [the longest x1 2.75 us: on_device(): jnp.sum(parts[:, :, model_width:2 * model_width].astype(F32), axis=0)]
  transfers between devices with their start and end apart: 13 -> 14, of which waited for: 8 -> 9; matrix products, arithmetic and copies ran while one was open for 22% -> 22% of each run, Pallas kernels for 0% -> 0%
where the time goes in v3:
time: 340 us; the launch traced here: 339 us
  waiting for transfers between devices  185 us (54%)
  matrix products  60.5 us (18%)
  starting transfers between devices  49.1 us (14%)
  local copies, waits for them, and re-layouts  15 us (4%)
  other arithmetic  14.7 us (4%)
  between operations  14.7 us (4%)
    dot_general x19, matrix products, dot(): lax.dot_general(left, right, (((lc,), (rc,)), ((), ())), preferred_elemen...  60.5 us
    all_to_all x5, waiting for transfers between devices, to_plane(): rows = lax.all_to_all(rows, PLANE, split_axis=0, concat_axis=0, tiled=True)  55.4 us
    ppermute x3, waiting for transfers between devices, placed(): other = lax.ppermute(own, 'z', [(i, i ^ N_Z // 2) for i in range(N_Z)])  52.3 us
    all_gather x1, waiting for transfers between devices, on_device(): lax.all_gather(jnp.concatenate([tokens, d_out, meta], axis=1), 'z', tiled...  42.4 us
    all_to_all x2, waiting for transfers between devices, to_column(): return lax.all_to_all(rows, 'z', split_axis=0, concat_axis=0, tiled=True)  34.5 us
    all_to_all x5, starting transfers between devices, to_plane(): rows = lax.all_to_all(rows, PLANE, split_axis=0, concat_axis=0, tiled=True)  23.1 us
    all_to_all x2, starting transfers between devices, to_column(): return lax.all_to_all(rows, 'z', split_axis=0, concat_axis=0, tiled=True)  13.4 us
    ppermute x3, starting transfers between devices, placed(): other = lax.ppermute(own, 'z', [(i, i ^ N_Z // 2) for i in range(N_Z)])  12.4 us
  transfers between devices with their start and end apart: 14, of which 9 were waited for; matrix products, arithmetic and copies ran while one was open for 22% of the time, Pallas kernels for 0%

profile of v3, /device:TPU:16, one launch (start us, length us, event | category | flops | bytes accessed | tf_op | source)
XLA Modules:
  0.0 338.6 jit_solution(17806027896697773613)
XLA Ops:
  7.2 0.8 convert_element_type.234
  8.2 0.7 fusion.68
  9.1 1.8 concatenate.9
  10.9 1.3 compare_select_fusion.3
  12.3 42.4 %all-gather.2.cloned.1.call-done = bf16[256,4224]{1,0:T(8,128)(2,1)} async-done(((bf16[32,4224]{1,0:T(8,128)(2,1)}), bf16[256,4224]{1,0:T(8,128)(2,1)}) %all-gather.2.cloned.1.call-update) | async-done | bytes 2162704 | tf_op jit(solution)/shard_map/all_gather | solution.py:43
  54.7 0.8 slice_convert_fusion.1
  55.6 0.9 fusion.85
  56.5 0.1 compare_reduce_fusion
  56.6 0.5 convolution_compare_fusion.1
  57.1 3.0 convolution_convert_fusion.4
  60.1 4.3 %all-to-all-start = ((bf16[8,48,2048]{2,1,0:T(8,128)(2,1)}), bf16[8,48,2048]{2,1,0:T(8,128)(2,1)}, u32[]{:S(2)}, u32[]{:S(2)}) async-start(bf16[8,48,2048]{2,1,0:T(8,128)(2,1)} %bitcast.74), calls=%async_computation | async-start | bytes 3145728 | tf_op jit(solution)/shard_map/all_to_all | solution.py:68
  64.4 1.0 copy.53
  65.4 1.0 copy.54
  66.4 0.8 fusion.54
  67.2 0.2 fusion.19
  67.4 3.0 multiply_convert_fusion
  70.4 15.6 %all-to-all-done = bf16[8,48,2048]{2,1,0:T(8,128)(2,1)} async-done(((bf16[8,48,2048]{2,1,0:T(8,128)(2,1)}), bf16[8,48,2048]{2,1,0:T(8,128)(2,1)}, u32[]{:S(2)}, u32[]{:S(2)}) %all-to-all-start) | async-done | bytes 1572896 | tf_op jit(solution)/shard_map/all_to_all | solution.py:68
  86.0 4.3 %all-to-all-start.3 = ((bf16[8,48,2048]{2,1,0:T(8,128)(2,1)}), bf16[8,48,2048]{2,1,0:T(8,128)(2,1)}, u32[]{:S(2)}, u32[]{:S(2)}) async-start(bf16[8,48,2048]{2,1,0:T(8,128)(2,1)} %bitcast.78), calls=%async_computation.3 | async-start | bytes 3145728 | tf_op jit(solution)/shard_map/all_to_all | solution.py:68
  90.4 3.7 %fusion.10 = f32[384,768]{1,0:T(8,128)S(1)} fusion(bf16[384,2048]{1,0:T(8,128)(2,1)} %bitcast.2, bf16[1,2048,768]{2,1,0:T(8,128)(2,1)} %param.11), kind=kOutput, calls=%fused_computation.13 | convolution fusion | flops 1207959552 | bytes 5898240 | tf_op jit(solution)/shard_map/dot_general | solution.py:13
  94.1 1.1 copy-done.13
  95.2 4.0 %multiply_convert_fusion.3 = (bf16[384,768]{1,0:T(8,128)(2,1)}, f32[384,768]{1,0:T(8,128)}) fusion(f32[384,768]{1,0:T(8,128)S(1)} %fusion.10, bf16[384,2048]{1,0:T(8,128)(2,1)} %bitcast.2, bf16[1,2048,768]{2,1,0:T(8,128)(2,1)S(1)} %copy-done), kind=kOutput, calls=%fused_computation.27 | convolution fusion | flops 1209729024 | bytes 7667712 | tf_op jit(solution)/shard_map/dot_general | solution.py:13
  99.2 12.6 %all-to-all-done.3 = bf16[8,48,2048]{2,1,0:T(8,128)(2,1)} async-done(((bf16[8,48,2048]{2,1,0:T(8,128)(2,1)}), bf16[8,48,2048]{2,1,0:T(8,128)(2,1)}, u32[]{:S(2)}, u32[]{:S(2)}) %all-to-all-start.3) | async-done | bytes 1572896 | tf_op jit(solution)/shard_map/all_to_all | solution.py:68
  111.9 5.0 %convolution_convert_fusion.2 = bf16[2048,768]{1,0:T(8,128)(2,1)} fusion(bf16[384,2048]{1,0:T(8,128)(2,1)} %bitcast.12, bf16[384,768]{1,0:T(8,128)(2,1)} %get-tuple-element.59), kind=kOutput, calls=%fused_computation.2 | convolution fusion | flops 1209532416 | bytes 5308416 | tf_op jit(solution)/shard_map/dot_general | solution.py:13
  117.0 0.6 copy-done.5
  117.6 0.1 compare_reduce_fusion.1
  117.7 0.2 fusion.23
  117.9 3.2 convolution_convert_fusion.3
  121.1 4.3 %all-to-all-start.6 = ((bf16[8,48,2048]{2,1,0:T(8,128)(2,1)}), bf16[8,48,2048]{2,1,0:T(8,128)(2,1)}, u32[]{:S(2)}, u32[]{:S(2)}) async-start(bf16[8,48,2048]{2,1,0:T(8,128)(2,1)} %bitcast.73), calls=%async_computation.6 | async-start | bytes 3145728 | tf_op jit(solution)/shard_map/all_to_all | solution.py:68
  125.4 5.9 %multiply_convert_fusion.2 = (bf16[384,768]{1,0:T(8,128)(2,1)}, bf16[384,768]{1,0:T(8,128)(2,1)}) fusion(f32[384,768]{1,0:T(8,128)} %copy-done.13, f32[384,768]{1,0:T(8,128)} %get-tuple-element.60, bf16[384,2048]{1,0:T(8,128)(2,1)} %bitcast.12, bf16[1,768,2048]{2,1,0:T(8,128)(2,1)} %param.13), kind=kOutput, calls=%fused_computation.26 | convolution fusion | flops 1211793408 | bytes 8257536 | tf_op jit(solution)/shard_map/dot_general | solution.py:13
  131.3 3.6 %collective-permute-start.1 = (bf16[384,768]{1,0:T(8,128)(2,1)}, bf16[384,768]{1,0:T(8,128)(2,1)}, u32[]{:S(2)}, u32[]{:S(2)}) collective-permute-start(bf16[384,768]{1,0:T(8,128)(2,1)} %get-tuple-element.48), channel_id=1, source_target_pairs={{0,32},{8,40},{16,48},{24,56},{32,0},{40,8},{48,16},{56,24},{1,33}... | collective-permute-start | bytes 1769480 | tf_op jit(solution)/shard_map/ppermute | solution.py:125
  134.9 0.6 dynamic_slice.7
  136.1 21.4 %collective-permute-done.1 = bf16[384,768]{1,0:T(8,128)(2,1)} collective-permute-done((bf16[384,768]{1,0:T(8,128)(2,1)}, bf16[384,768]{1,0:T(8,128)(2,1)}, u32[]{:S(2)}, u32[]{:S(2)}) %collective-permute-start.1) | collective-permute-done | bytes 589856 | tf_op jit(solution)/shard_map/ppermute | solution.py:125
  157.6 5.1 %convolution_convert_fusion = bf16[2048,768]{1,0:T(8,128)(2,1)} fusion(bf16[384,2048]{1,0:T(8,128)(2,1)} %bitcast.19, bf16[384,768]{1,0:T(8,128)(2,1)} %collective-permute-done.1, bf16[384,768]{1,0:T(8,128)(2,1)} %get-tuple-element.48, pred[]{:T(512)} %bitcast.20), kind=kOutput, calls=%fused_computation | convolution fusion | flops 1209827328 | bytes 5898241 | tf_op jit(solution)/shard_map/dot_general | solution.py:13
  162.7 2.6 fusion.4
  165.3 2.6 add_convert_fusion
  167.9 5.9 %all-to-all-start.4 = ((bf16[8,48,2048]{2,1,0:T(8,128)(2,1)}), bf16[8,48,2048]{2,1,0:T(8,128)(2,1)}, u32[]{:S(2)}, u32[]{:S(2)}) async-start(bf16[8,48,2048]{2,1,0:T(8,128)(2,1)} %bitcast.79), calls=%async_computation.4 | async-start | bytes 3145728 | tf_op jit(solution)/shard_map/all_to_all | solution.py:68
  173.8 3.0 collective-permute-start
  176.8 4.7 %fusion.14 = bf16[384,2048]{1,0:T(8,128)(2,1)} fusion(bf16[384,768]{1,0:T(8,128)(2,1)} %get-tuple-element.59, bf16[1,768,2048]{2,1,0:T(8,128)(2,1)} %param.13), kind=kOutput, calls=%fused_computation.18 | convolution fusion | flops 1208745984 | bytes 5308416 | tf_op jit(solution)/shard_map/dot_general | solution.py:13
  181.5 14.0 %all-to-all-done.4 = bf16[8,48,2048]{2,1,0:T(8,128)(2,1)} async-done(((bf16[8,48,2048]{2,1,0:T(8,128)(2,1)}), bf16[8,48,2048]{2,1,0:T(8,128)(2,1)}, u32[]{:S(2)}, u32[]{:S(2)}) %all-to-all-start.4) | async-done | bytes 1572896 | tf_op jit(solution)/shard_map/all_to_all | solution.py:68
  195.4 4.3 %all-to-all-start.1 = ((bf16[8,48,2048]{2,1,0:T(8,128)(2,1)}), bf16[8,48,2048]{2,1,0:T(8,128)(2,1)}, u32[]{:S(2)}, u32[]{:S(2)}) async-start(bf16[8,48,2048]{2,1,0:T(8,128)(2,1)} %bitcast.77), calls=%async_computation.1 | async-start | bytes 3145728 | tf_op jit(solution)/shard_map/all_to_all | solution.py:68
  199.8 5.1 %convolution_convert_fusion.1 = bf16[2048,768]{1,0:T(8,128)(2,1)} fusion(bf16[384,2048]{1,0:T(8,128)(2,1)} %bitcast.19, bf16[384,768]{1,0:T(8,128)(2,1)} %collective-permute-done, bf16[384,768]{1,0:T(8,128)(2,1)} %get-tuple-element.47, pred[]{:T(512)} %bitcast.20), kind=kOutput, calls=%fused_computation.1 | convolution fusion | flops 1209827328 | bytes 5898241 | tf_op jit(solution)/shard_map/dot_general | solution.py:13
  204.9 3.2 convolution_convert_fusion.5
  208.1 13.2 %all-to-all-done.1 = bf16[8,48,2048]{2,1,0:T(8,128)(2,1)} async-done(((bf16[8,48,2048]{2,1,0:T(8,128)(2,1)}), bf16[8,48,2048]{2,1,0:T(8,128)(2,1)}, u32[]{:S(2)}, u32[]{:S(2)}) %all-to-all-start.1) | async-done | bytes 1572896 | tf_op jit(solution)/shard_map/all_to_all | solution.py:68
  221.3 9.2 %all-to-all-start.5 = ((bf16[8,32,2048]{2,1,0:T(8,128)(2,1)}), bf16[8,32,2048]{2,1,0:T(8,128)(2,1)}, u32[]{:S(2)}, u32[]{:S(2)}) async-start(bf16[8,32,2048]{2,1,0:T(8,128)(2,1)} %bitcast.76), calls=%async_computation.5 | async-start | bytes 2097152 | tf_op jit(solution)/shard_map/all_to_all | solution.py:73
  230.4 3.1 convolution_multiply_fusion
  233.6 1.9 copy.56
  235.5 1.8 select_reduce_fusion
  237.4 0.1 copy.61
  237.6 0.1 copy.60
  237.7 0.1 copy.59
  237.8 2.3 fusion.38
  240.1 3.3 fusion.17
  243.3 3.1 concatenate.11
  246.4 12.6 %all-to-all-done.5 = bf16[8,32,2048]{2,1,0:T(8,128)(2,1)} async-done(((bf16[8,32,2048]{2,1,0:T(8,128)(2,1)}), bf16[8,32,2048]{2,1,0:T(8,128)(2,1)}, u32[]{:S(2)}, u32[]{:S(2)}) %all-to-all-start.5) | async-done | bytes 1048608 | tf_op jit(solution)/shard_map/all_to_all | solution.py:73
  259.0 4.3 %all-to-all-start.2 = ((bf16[8,32,2176]{2,1,0:T(8,128)(2,1)}), bf16[8,32,2176]{2,1,0:T(8,128)(2,1)}, u32[]{:S(2)}, u32[]{:S(2)}) async-start(bf16[8,32,2176]{2,1,0:T(8,128)(2,1)} %bitcast.75), calls=%async_computation.2 | async-start | bytes 2228224 | tf_op jit(solution)/shard_map/all_to_all | solution.py:73
  263.2 2.1 fusion.45
  265.3 5.8 %collective-permute-start.2 = (bf16[512,768]{1,0:T(8,128)(2,1)}, bf16[512,768]{1,0:T(8,128)(2,1)}, u32[]{:S(2)}, u32[]{:S(2)}) collective-permute-start(bf16[512,768]{1,0:T(8,128)(2,1)} %reduce-scatter.8.cloned.1.call-done), channel_id=1, source_target_pairs={{0,32},{8,40},{16,48},{24,56},{32,0},{40,8},{48,16},{56,24},{1,33}... | collective-permute-start | bytes 2359304 | tf_op jit(solution)/shard_map/ppermute | solution.py:125
  271.1 21.9 %all-to-all-done.2 = bf16[8,32,2176]{2,1,0:T(8,128)(2,1)} async-done(((bf16[8,32,2176]{2,1,0:T(8,128)(2,1)}), bf16[8,32,2176]{2,1,0:T(8,128)(2,1)}, u32[]{:S(2)}, u32[]{:S(2)}) %all-to-all-start.2) | async-done | bytes 1114144 | tf_op jit(solution)/shard_map/all_to_all | solution.py:73
  293.0 0.8 add_bitcast_fusion
  293.9 0.7 copy.63
  294.6 2.1 fusion.44
  296.8 30.9 %collective-permute-done.2 = bf16[512,768]{1,0:T(8,128)(2,1)} collective-permute-done((bf16[512,768]{1,0:T(8,128)(2,1)}, bf16[512,768]{1,0:T(8,128)(2,1)}, u32[]{:S(2)}, u32[]{:S(2)}) %collective-permute-start.2) | collective-permute-done | bytes 786464 | tf_op jit(solution)/shard_map/ppermute | solution.py:125
  327.6 2.1 select_bitcast_fusion
  329.8 2.3 copy.64
  (55 shorter events, 1.0 us)
Async XLA Ops:
  7.2 88.1 %copy-start = (bf16[1,2048,768]{2,1,0:T(8,128)(2,1)S(1)}, bf16[1,2048,768]{2,1,0:T(8,128)(2,1)}, u32[]{:S(2)}) copy-start(bf16[1,2048,768]{2,1,0:T(8,128)(2,1)} %param.12) | copy-start | bytes 9437188
  7.2 47.5 %all-gather.2.cloned.1.call-start = ((), (), s32[]{:S(2)}) async-start(), calls=%async_computation.10 | async-start | bytes 2433024 | tf_op jit(solution)/shard_map/all_gather | solution.py:43
  12.2 47.8 %copy-start.4 = (s32[8]{0:T(128)}, s32[8]{0:T(128)S(1)}, u32[]{:S(2)}) copy-start(s32[8]{0:T(128)S(1)} %get-tuple-element.62) | copy-start | bytes 100
  12.3 47.8 %copy-start.6 = (s32[256]{0:T(256)}, s32[256]{0:T(256)S(1)}, u32[]{:S(2)}) copy-start(s32[256]{0:T(256)S(1)} %get-tuple-element.65) | copy-start | bytes 3076
  12.3 47.8 %copy-start.8 = (f32[256]{0:T(256)}, f32[256]{0:T(256)S(1)}, u32[]{:S(2)}) copy-start(f32[256]{0:T(256)S(1)} %get-tuple-element.66) | copy-start | bytes 3076
  12.3 47.8 %copy-start.2 = (f32[384]{0:T(512)}, f32[384]{0:T(512)S(1)}, u32[]{:S(2)}) copy-start(f32[384]{0:T(512)S(1)} %get-tuple-element.64) | copy-start | bytes 4612
  60.1 25.9 %all-to-all-start = ((bf16[8,48,2048]{2,1,0:T(8,128)(2,1)}), bf16[8,48,2048]{2,1,0:T(8,128)(2,1)}, u32[]{:S(2)}, u32[]{:S(2)}) async-start(bf16[8,48,2048]{2,1,0:T(8,128)(2,1)} %bitcast.74), calls=%async_computation | async-start | bytes 3145728 | tf_op jit(solution)/shard_map/all_to_all | solution.py:68
  86.0 25.9 %all-to-all-start.3 = ((bf16[8,48,2048]{2,1,0:T(8,128)(2,1)}), bf16[8,48,2048]{2,1,0:T(8,128)(2,1)}, u32[]{:S(2)}, u32[]{:S(2)}) async-start(bf16[8,48,2048]{2,1,0:T(8,128)(2,1)} %bitcast.78), calls=%async_computation.3 | async-start | bytes 3145728 | tf_op jit(solution)/shard_map/all_to_all | solution.py:68
  90.3 175.0 %reduce-scatter.8.cloned.1.call-start = ((), (), s32[]{:S(2)}) async-start(), calls=%async_computation.13 | async-start | bytes 3932160 | tf_op jit(solution)/shard_map/reduce_scatter | solution.py:129
  94.1 1.1 copy-start.13
  116.9 0.7 copy-start.5
  116.9 0.8 copy-start.7
  116.9 0.8 copy-start.9
  116.9 1.0 copy-start.3
  121.1 36.5 %all-to-all-start.6 = ((bf16[8,48,2048]{2,1,0:T(8,128)(2,1)}), bf16[8,48,2048]{2,1,0:T(8,128)(2,1)}, u32[]{:S(2)}, u32[]{:S(2)}) async-start(bf16[8,48,2048]{2,1,0:T(8,128)(2,1)} %bitcast.73), calls=%async_computation.6 | async-start | bytes 3145728 | tf_op jit(solution)/shard_map/all_to_all | solution.py:68
  125.4 206.7 %reduce-scatter.6.cloned.1.call-start = ((), (), s32[]{:S(2)}) async-start(), calls=%async_computation.12 | async-start | bytes 3932160 | tf_op jit(solution)/shard_map/reduce_scatter | solution.py:129
  125.4 9.5 %copy-start.10 = (s32[64]{0:T(128)S(1)}, s32[64]{0:T(128)}, u32[]{:S(2)}) copy-start(s32[64]{0:T(128)} %param.14) | copy-start | bytes 772
  131.3 26.2 %collective-permute-start.1 = (bf16[384,768]{1,0:T(8,128)(2,1)}, bf16[384,768]{1,0:T(8,128)(2,1)}, u32[]{:S(2)}, u32[]{:S(2)}) collective-permute-start(bf16[384,768]{1,0:T(8,128)(2,1)} %get-tuple-element.48), channel_id=1, source_target_pairs={{0,32},{8,40},{16,48},{24,56},{32,0},{40,8},{48,16},{56,24},{1,33}... | collective-permute-start | bytes 1769480 | tf_op jit(solution)/shard_map/ppermute | solution.py:125
  162.6 2.7 copy-start.11
  162.6 2.7 copy-start.12
  167.9 27.5 %all-to-all-start.4 = ((bf16[8,48,2048]{2,1,0:T(8,128)(2,1)}), bf16[8,48,2048]{2,1,0:T(8,128)(2,1)}, u32[]{:S(2)}, u32[]{:S(2)}) async-start(bf16[8,48,2048]{2,1,0:T(8,128)(2,1)} %bitcast.79), calls=%async_computation.4 | async-start | bytes 3145728 | tf_op jit(solution)/shard_map/all_to_all | solution.py:68
  173.8 26.0 %collective-permute-start = (bf16[384,768]{1,0:T(8,128)(2,1)}, bf16[384,768]{1,0:T(8,128)(2,1)}, u32[]{:S(2)}, u32[]{:S(2)}) collective-permute-start(bf16[384,768]{1,0:T(8,128)(2,1)} %get-tuple-element.47), channel_id=1, source_target_pairs={{0,32},{8,40},{16,48},{24,56},{32,0},{40,8},{48,16},{56,24},{1,33}... | collective-permute-start | bytes 1769480 | tf_op jit(solution)/shard_map/ppermute | solution.py:125
  195.4 25.9 %all-to-all-start.1 = ((bf16[8,48,2048]{2,1,0:T(8,128)(2,1)}), bf16[8,48,2048]{2,1,0:T(8,128)(2,1)}, u32[]{:S(2)}, u32[]{:S(2)}) async-start(bf16[8,48,2048]{2,1,0:T(8,128)(2,1)} %bitcast.77), calls=%async_computation.1 | async-start | bytes 3145728 | tf_op jit(solution)/shard_map/all_to_all | solution.py:68
  199.7 132.3 %reduce-scatter.4.cloned.1.call-start = ((), (), s32[]{:S(2)}) async-start(), calls=%async_computation.11 | async-start | bytes 3932160 | tf_op jit(solution)/shard_map/reduce_scatter | solution.py:129
  221.3 37.7 %all-to-all-start.5 = ((bf16[8,32,2048]{2,1,0:T(8,128)(2,1)}), bf16[8,32,2048]{2,1,0:T(8,128)(2,1)}, u32[]{:S(2)}, u32[]{:S(2)}) async-start(bf16[8,32,2048]{2,1,0:T(8,128)(2,1)} %bitcast.76), calls=%async_computation.5 | async-start | bytes 2097152 | tf_op jit(solution)/shard_map/all_to_all | solution.py:73
  259.0 34.1 %all-to-all-start.2 = ((bf16[8,32,2176]{2,1,0:T(8,128)(2,1)}), bf16[8,32,2176]{2,1,0:T(8,128)(2,1)}, u32[]{:S(2)}, u32[]{:S(2)}) async-start(bf16[8,32,2176]{2,1,0:T(8,128)(2,1)} %bitcast.75), calls=%async_computation.2 | async-start | bytes 2228224 | tf_op jit(solution)/shard_map/all_to_all | solution.py:73
  265.3 62.3 %collective-permute-start.2 = (bf16[512,768]{1,0:T(8,128)(2,1)}, bf16[512,768]{1,0:T(8,128)(2,1)}, u32[]{:S(2)}, u32[]{:S(2)}) collective-permute-start(bf16[512,768]{1,0:T(8,128)(2,1)} %reduce-scatter.8.cloned.1.call-done), channel_id=1, source_target_pairs={{0,32},{8,40},{16,48},{24,56},{32,0},{40,8},{48,16},{56,24},{1,33}... | collective-permute-start | bytes 2359304 | tf_op jit(solution)/shard_map/ppermute | solution.py:125
  294.6 33.0 %copy-start.1 = (bf16[512,768]{1,0:T(8,128)(2,1)S(1)}, bf16[512,768]{1,0:T(8,128)(2,1)}, u32[]{:S(2)}) copy-start(bf16[512,768]{1,0:T(8,128)(2,1)} %reduce-scatter.8.cloned.1.call-done) | copy-start | bytes 2359300
Sparse Core Ops, SparseCore 0:
  11.0 43.6 all-gather.1
  117.0 36.2 reduce-scatter.7
  162.8 44.3 reduce-scatter.5
  210.2 41.4 reduce-scatter.3

commit v4 on v2

--- a/solution.py
+++ b/solution.py
@@ -146,13 +146,16 @@
     back_rows = to_plane(d_rows)
     dtok_part = dot(pick, back_rows, 0, 0).astype(BF16)
     parts = to_column(jnp.concatenate([mix_part, dtok_part, padded(split3(dg_part), 128)], axis=1))
-    mixture = jnp.sum(parts[:, :, :model_width].astype(F32), axis=0).astype(BF16)
-    d_tokens = jnp.sum(
-        parts[:, :, model_width : 2 * model_width].astype(F32), axis=0
-    ).astype(BF16)
-    dg_sum = jnp.sum(
-        parts[:, :, 2 * model_width : 2 * model_width + 3 * top_count].astype(F32), axis=0
-    )
+
+    def summed(first, width):
+        planes = [parts[i, :, first : first + width].astype(F32) for i in range(N_Z)]
+        while len(planes) > 1:
+            planes = [x + y for x, y in zip(planes[::2], planes[1::2])]
+        return planes[0]
+
+    mixture = summed(0, model_width).astype(BF16)
+    d_tokens = summed(model_width, model_width).astype(BF16)
+    dg_sum = summed(2 * model_width, 3 * top_count)
     d_gates = (
         dg_sum[:, :top_count]
         + dg_sum[:, top_count : 2 * top_count]

time: 340 us -> 340 us (level)
    reduce_sum x2 -> x0, other arithmetic: 3.61 us -> none  [the longest x1 2.75 us: on_device(): jnp.sum(parts[:, :, model_width:2 * model_width].astype(F32), axis=0)]
    add x0 -> x2, other arithmetic: none -> 3.53 us  [summed(): planes = [x + y for x, y in zip(planes[::2], planes[1::2])]]
where the time goes in v4:
time: 340 us; the launch traced here: 339 us
  waiting for transfers between devices  191 us (56%)
  matrix products  60 us (18%)
  starting transfers between devices  43.8 us (13%)
  local copies, waits for them, and re-layouts  16.5 us (5%)
  between operations  14.7 us (4%)
  other arithmetic  13.1 us (4%)
    dot_general x19, matrix products, dot(): lax.dot_general(left, right, (((lc,), (rc,)), ((), ())), preferred_elemen...  60 us
    ppermute x3, waiting for transfers between devices, placed(): other = lax.ppermute(own, 'z', [(i, i ^ N_Z // 2) for i in range(N_Z)])  53.9 us
    all_to_all x5, waiting for transfers between devices, to_plane(): rows = lax.all_to_all(rows, PLANE, split_axis=0, concat_axis=0, tiled=True)  50.1 us
    all_to_all x1, waiting for transfers between devices, to_column(): return lax.all_to_all(rows, 'z', split_axis=0, concat_axis=0, tiled=True)  43.9 us
    all_gather x1, waiting for transfers between devices, on_device(): lax.all_gather(jnp.concatenate([tokens, d_out, meta], axis=1), 'z', tiled...  42.5 us
    all_to_all x5, starting transfers between devices, to_plane(): rows = lax.all_to_all(rows, PLANE, split_axis=0, concat_axis=0, tiled=True)  21.5 us
    ppermute x3, starting transfers between devices, placed(): other = lax.ppermute(own, 'z', [(i, i ^ N_Z // 2) for i in range(N_Z)])  11.3 us
    all_to_all x1, starting transfers between devices, to_column(): return lax.all_to_all(rows, 'z', split_axis=0, concat_axis=0, tiled=True)  10.8 us
  transfers between devices with their start and end apart: 13, of which 8 were waited for; matrix products, arithmetic and copies ran while one was open for 22% of the time, Pallas kernels for 0%

profile of v4, /device:TPU:16, one launch (start us, length us, event | category | flops | bytes accessed | tf_op | source)
XLA Modules:
  0.0 338.6 jit_solution(2725589456345637908)
XLA Ops:
  7.2 0.8 convert_element_type.234
  8.1 0.1 copy.47
  8.2 0.7 fusion.68
  8.9 0.1 copy.50
  8.9 0.1 copy.49
  9.1 1.8 concatenate.9
  10.9 1.3 compare_select_fusion.3
  12.2 42.5 %all-gather.2.cloned.1.call-done = bf16[256,4224]{1,0:T(8,128)(2,1)} async-done(((bf16[32,4224]{1,0:T(8,128)(2,1)}), bf16[256,4224]{1,0:T(8,128)(2,1)}) %all-gather.2.cloned.1.call-update) | async-done | bytes 2162704 | tf_op jit(solution)/shard_map/all_gather | solution.py:43
  54.7 0.8 slice_convert_fusion.1
  55.6 0.9 fusion.85
  56.5 0.1 compare_reduce_fusion
  56.6 0.5 convolution_compare_fusion.1
  57.1 3.0 convolution_convert_fusion.4
  60.1 4.3 %all-to-all-start = ((bf16[8,48,2048]{2,1,0:T(8,128)(2,1)}), bf16[8,48,2048]{2,1,0:T(8,128)(2,1)}, u32[]{:S(2)}, u32[]{:S(2)}) async-start(bf16[8,48,2048]{2,1,0:T(8,128)(2,1)} %bitcast.74), calls=%async_computation | async-start | bytes 3145728 | tf_op jit(solution)/shard_map/all_to_all | solution.py:68
  64.4 1.0 copy.53
  65.4 1.0 copy.54
  66.4 0.8 fusion.54
  67.2 0.2 fusion.19
  67.4 3.0 multiply_convert_fusion
  70.4 15.6 %all-to-all-done = bf16[8,48,2048]{2,1,0:T(8,128)(2,1)} async-done(((bf16[8,48,2048]{2,1,0:T(8,128)(2,1)}), bf16[8,48,2048]{2,1,0:T(8,128)(2,1)}, u32[]{:S(2)}, u32[]{:S(2)}) %all-to-all-start) | async-done | bytes 1572896 | tf_op jit(solution)/shard_map/all_to_all | solution.py:68
  86.0 4.3 %all-to-all-start.2 = ((bf16[8,48,2048]{2,1,0:T(8,128)(2,1)}), bf16[8,48,2048]{2,1,0:T(8,128)(2,1)}, u32[]{:S(2)}, u32[]{:S(2)}) async-start(bf16[8,48,2048]{2,1,0:T(8,128)(2,1)} %bitcast.76), calls=%async_computation.2 | async-start | bytes 3145728 | tf_op jit(solution)/shard_map/all_to_all | solution.py:68
  90.4 3.9 %fusion.10 = f32[384,768]{1,0:T(8,128)S(1)} fusion(bf16[384,2048]{1,0:T(8,128)(2,1)} %bitcast.2, bf16[1,2048,768]{2,1,0:T(8,128)(2,1)} %param.11), kind=kOutput, calls=%fused_computation.13 | convolution fusion | flops 1207959552 | bytes 5898240 | tf_op jit(solution)/shard_map/dot_general | solution.py:13
  94.3 1.1 copy-done.14
  95.3 4.0 %multiply_convert_fusion.3 = (bf16[384,768]{1,0:T(8,128)(2,1)}, f32[384,768]{1,0:T(8,128)}) fusion(f32[384,768]{1,0:T(8,128)S(1)} %fusion.10, bf16[384,2048]{1,0:T(8,128)(2,1)} %bitcast.2, bf16[1,2048,768]{2,1,0:T(8,128)(2,1)S(1)} %copy-done.11), kind=kOutput, calls=%fused_computation.27 | convolution fusion | flops 1209729024 | bytes 7667712 | tf_op jit(solution)/shard_map/dot_general | solution.py:13
  99.4 12.5 %all-to-all-done.2 = bf16[8,48,2048]{2,1,0:T(8,128)(2,1)} async-done(((bf16[8,48,2048]{2,1,0:T(8,128)(2,1)}), bf16[8,48,2048]{2,1,0:T(8,128)(2,1)}, u32[]{:S(2)}, u32[]{:S(2)}) %all-to-all-start.2) | async-done | bytes 1572896 | tf_op jit(solution)/shard_map/all_to_all | solution.py:68
  111.8 5.0 %convolution_convert_fusion = bf16[2048,768]{1,0:T(8,128)(2,1)} fusion(bf16[384,2048]{1,0:T(8,128)(2,1)} %bitcast.9, bf16[384,768]{1,0:T(8,128)(2,1)} %get-tuple-element.57), kind=kOutput, calls=%fused_computation | convolution fusion | flops 1209532416 | bytes 5308416 | tf_op jit(solution)/shard_map/dot_general | solution.py:13
  117.0 0.5 copy-done.5
  117.5 0.1 compare_reduce_fusion.1
  117.6 0.2 fusion.23
  117.8 3.2 convolution_convert_fusion.3
  121.0 4.3 %all-to-all-start.5 = ((bf16[8,48,2048]{2,1,0:T(8,128)(2,1)}), bf16[8,48,2048]{2,1,0:T(8,128)(2,1)}, u32[]{:S(2)}, u32[]{:S(2)}) async-start(bf16[8,48,2048]{2,1,0:T(8,128)(2,1)} %bitcast.73), calls=%async_computation.5 | async-start | bytes 3145728 | tf_op jit(solution)/shard_map/all_to_all | solution.py:68
  125.4 5.0 %multiply_convert_fusion.2 = (bf16[384,768]{1,0:T(8,128)(2,1)}, bf16[384,768]{1,0:T(8,128)(2,1)}) fusion(f32[384,768]{1,0:T(8,128)} %copy-done.14, f32[384,768]{1,0:T(8,128)} %get-tuple-element.58, bf16[384,2048]{1,0:T(8,128)(2,1)} %bitcast.9, bf16[1,768,2048]{2,1,0:T(8,128)(2,1)S(1)} %copy-done), kind=kOutput, calls=%fused_computation.26 | convolution fusion | flops 1211793408 | bytes 8257536 | tf_op jit(solution)/shard_map/dot_general | solution.py:13
  130.4 3.0 collective-permute-start.1
  133.4 0.6 dynamic_slice.7
  134.7 21.7 %collective-permute-done.1 = bf16[384,768]{1,0:T(8,128)(2,1)} collective-permute-done((bf16[384,768]{1,0:T(8,128)(2,1)}, bf16[384,768]{1,0:T(8,128)(2,1)}, u32[]{:S(2)}, u32[]{:S(2)}) %collective-permute-start.1) | collective-permute-done | bytes 589856 | tf_op jit(solution)/shard_map/ppermute | solution.py:123
  156.3 5.1 %convolution_convert_fusion.1 = bf16[2048,768]{1,0:T(8,128)(2,1)} fusion(bf16[384,2048]{1,0:T(8,128)(2,1)} %bitcast.18, bf16[384,768]{1,0:T(8,128)(2,1)} %collective-permute-done.1, bf16[384,768]{1,0:T(8,128)(2,1)} %get-tuple-element.44, pred[]{:T(512)} %bitcast.19), kind=kOutput, calls=%fused_computation.1 | convolution fusion | flops 1209827328 | bytes 5898241 | tf_op jit(solution)/shard_map/dot_general | solution.py:13
  161.4 3.6 %fusion.14 = bf16[384,2048]{1,0:T(8,128)(2,1)} fusion(bf16[384,768]{1,0:T(8,128)(2,1)} %get-tuple-element.57, bf16[1,768,2048]{2,1,0:T(8,128)(2,1)S(1)} %copy-done), kind=kOutput, calls=%fused_computation.18 | convolution fusion | flops 1208745984 | bytes 5308416 | tf_op jit(solution)/shard_map/dot_general | solution.py:13
  165.0 4.3 %all-to-all-start.1 = ((bf16[8,48,2048]{2,1,0:T(8,128)(2,1)}), bf16[8,48,2048]{2,1,0:T(8,128)(2,1)}, u32[]{:S(2)}, u32[]{:S(2)}) async-start(bf16[8,48,2048]{2,1,0:T(8,128)(2,1)} %bitcast.77), calls=%async_computation.1 | async-start | bytes 3145728 | tf_op jit(solution)/shard_map/all_to_all | solution.py:68
  169.4 2.4 collective-permute-start
  171.8 3.5 %fusion.4 = f32[384,2048]{1,0:T(8,128)S(1)} fusion(bf16[384,768]{1,0:T(8,128)(2,1)} %get-tuple-element.44, bf16[1,2048,768]{2,1,0:T(8,128)(2,1)} %param.12), kind=kOutput, calls=%fused_computation.7 | convolution fusion | flops 1207959552 | bytes 6881280 | tf_op jit(solution)/shard_map/dot_general | solution.py:13
  175.3 2.6 add_convert_fusion
  177.9 13.0 %all-to-all-done.1 = bf16[8,48,2048]{2,1,0:T(8,128)(2,1)} async-done(((bf16[8,48,2048]{2,1,0:T(8,128)(2,1)}), bf16[8,48,2048]{2,1,0:T(8,128)(2,1)}, u32[]{:S(2)}, u32[]{:S(2)}) %all-to-all-start.1) | async-done | bytes 1572896 | tf_op jit(solution)/shard_map/all_to_all | solution.py:68
  190.9 4.3 %all-to-all-start.3 = ((bf16[8,48,2048]{2,1,0:T(8,128)(2,1)}), bf16[8,48,2048]{2,1,0:T(8,128)(2,1)}, u32[]{:S(2)}, u32[]{:S(2)}) async-start(bf16[8,48,2048]{2,1,0:T(8,128)(2,1)} %bitcast.75), calls=%async_computation.3 | async-start | bytes 3145728 | tf_op jit(solution)/shard_map/all_to_all | solution.py:68
  195.3 3.1 convolution_multiply_fusion
  198.4 1.9 copy.56
  200.3 5.1 %convolution_convert_fusion.2 = bf16[2048,768]{1,0:T(8,128)(2,1)} fusion(bf16[384,2048]{1,0:T(8,128)(2,1)} %bitcast.18, bf16[384,768]{1,0:T(8,128)(2,1)} %collective-permute-done, bf16[384,768]{1,0:T(8,128)(2,1)} %get-tuple-element.43, pred[]{:T(512)} %bitcast.19), kind=kOutput, calls=%fused_computation.2 | convolution fusion | flops 1209827328 | bytes 5898241 | tf_op jit(solution)/shard_map/dot_general | solution.py:13
  205.5 1.8 select_reduce_fusion
  207.4 0.1 copy.61
  207.5 0.1 copy.60
  207.6 0.1 copy.59
  207.7 9.0 %all-to-all-done.3 = bf16[8,48,2048]{2,1,0:T(8,128)(2,1)} async-done(((bf16[8,48,2048]{2,1,0:T(8,128)(2,1)}), bf16[8,48,2048]{2,1,0:T(8,128)(2,1)}, u32[]{:S(2)}, u32[]{:S(2)}) %all-to-all-start.3) | async-done | bytes 1572896 | tf_op jit(solution)/shard_map/all_to_all | solution.py:68
  216.8 3.1 convolution_convert_fusion.5
  219.9 2.2 fusion.38
  222.2 3.7 %fusion.17 = bf16[256,2048]{1,0:T(8,128)(2,1)} fusion(f32[256,2048]{1,0:T(8,128)S(1)} %fusion.38, bf16[384,2048]{1,0:T(8,128)(2,1)} %bitcast.7, pred[384,256]{1,0:T(32,128)(4,1)S(1)} %convolution_compare_fusion.1, f32[384]{0:T(512)S(1)} %fusion.19), kind=kOutput, calls=%fused_computation.23 | convolution fusion | flops 404488192 | bytes 4818432 | tf_op jit(solution)/shard_map/dot_general | solution.py:13
  225.8 4.7 %concatenate.11 = bf16[256,4224]{1,0:T(8,128)(2,1)} concatenate(bf16[256,2048]{1,0:T(8,128)(2,1)} %fusion.17, bf16[256,2048]{1,0:T(8,128)(2,1)} %convolution_convert_fusion.5, bf16[256,8]{1,0:T(8,128)(2,1)S(1)} %copy.59, bf16[256,8]{1,0:T(8,128)(2,1)S(1)} %copy.60, bf16[256,8]{1,0:T(8,128)(2,1)S(1)} %copy.61, bf16[256,104]{1,0:T(8,128)(2,1)S(1)} %broadcast_in_dim.94), dimensions={1} | concatenate | bytes 4325376 | tf_op jit(solution)/shard_map/concatenate | solution.py:148
  230.5 10.8 %all-to-all-start.4 = ((bf16[8,32,4224]{2,1,0:T(8,128)(2,1)}), bf16[8,32,4224]{2,1,0:T(8,128)(2,1)}, u32[]{:S(2)}, u32[]{:S(2)}) async-start(bf16[8,32,4224]{2,1,0:T(8,128)(2,1)} %bitcast.72), calls=%async_computation.4 | async-start | bytes 4325376 | tf_op jit(solution)/shard_map/all_to_all | solution.py:73
  241.3 5.9 %collective-permute-start.2 = (bf16[512,768]{1,0:T(8,128)(2,1)}, bf16[512,768]{1,0:T(8,128)(2,1)}, u32[]{:S(2)}, u32[]{:S(2)}) collective-permute-start(bf16[512,768]{1,0:T(8,128)(2,1)} %reduce-scatter.8.cloned.1.call-done), channel_id=1, source_target_pairs={{0,32},{8,40},{16,48},{24,56},{32,0},{40,8},{48,16},{56,24},{1,33}... | collective-permute-start | bytes 2359304 | tf_op jit(solution)/shard_map/ppermute | solution.py:123
  247.2 43.9 %all-to-all-done.4 = bf16[8,32,4224]{2,1,0:T(8,128)(2,1)} async-done(((bf16[8,32,4224]{2,1,0:T(8,128)(2,1)}), bf16[8,32,4224]{2,1,0:T(8,128)(2,1)}, u32[]{:S(2)}, u32[]{:S(2)}) %all-to-all-start.4) | async-done | bytes 2162720 | tf_op jit(solution)/shard_map/all_to_all | solution.py:73
  291.1 0.8 add_bitcast_fusion
  292.0 0.7 copy.63
  292.7 2.7 fusion.45
  295.4 32.3 %collective-permute-done.2 = bf16[512,768]{1,0:T(8,128)(2,1)} collective-permute-done((bf16[512,768]{1,0:T(8,128)(2,1)}, bf16[512,768]{1,0:T(8,128)(2,1)}, u32[]{:S(2)}, u32[]{:S(2)}) %collective-permute-start.2) | collective-permute-done | bytes 786464 | tf_op jit(solution)/shard_map/ppermute | solution.py:123
  327.7 2.1 select_bitcast_fusion
  329.8 2.3 copy.64
  (54 shorter events, 0.8 us)
Async XLA Ops:
  7.2 118.2 %copy-start = (bf16[1,768,2048]{2,1,0:T(8,128)(2,1)S(1)}, bf16[1,768,2048]{2,1,0:T(8,128)(2,1)}, u32[]{:S(2)}) copy-start(bf16[1,768,2048]{2,1,0:T(8,128)(2,1)} %param.13) | copy-start | bytes 9437188
  7.2 47.5 %all-gather.2.cloned.1.call-start = ((), (), s32[]{:S(2)}) async-start(), calls=%async_computation.9 | async-start | bytes 2433024 | tf_op jit(solution)/shard_map/all_gather | solution.py:43
  12.2 47.8 %copy-start.4 = (s32[8]{0:T(128)}, s32[8]{0:T(128)S(1)}, u32[]{:S(2)}) copy-start(s32[8]{0:T(128)S(1)} %get-tuple-element.60) | copy-start | bytes 100
  12.2 47.8 %copy-start.6 = (s32[256]{0:T(256)}, s32[256]{0:T(256)S(1)}, u32[]{:S(2)}) copy-start(s32[256]{0:T(256)S(1)} %get-tuple-element.63) | copy-start | bytes 3076
  12.2 47.8 %copy-start.8 = (f32[256]{0:T(256)}, f32[256]{0:T(256)S(1)}, u32[]{:S(2)}) copy-start(f32[256]{0:T(256)S(1)} %get-tuple-element.64) | copy-start | bytes 3076
  12.2 47.8 %copy-start.2 = (f32[384]{0:T(512)}, f32[384]{0:T(512)S(1)}, u32[]{:S(2)}) copy-start(f32[384]{0:T(512)S(1)} %get-tuple-element.62) | copy-start | bytes 4612
  60.1 25.9 %all-to-all-start = ((bf16[8,48,2048]{2,1,0:T(8,128)(2,1)}), bf16[8,48,2048]{2,1,0:T(8,128)(2,1)}, u32[]{:S(2)}, u32[]{:S(2)}) async-start(bf16[8,48,2048]{2,1,0:T(8,128)(2,1)} %bitcast.74), calls=%async_computation | async-start | bytes 3145728 | tf_op jit(solution)/shard_map/all_to_all | solution.py:68
  86.0 25.9 %all-to-all-start.2 = ((bf16[8,48,2048]{2,1,0:T(8,128)(2,1)}), bf16[8,48,2048]{2,1,0:T(8,128)(2,1)}, u32[]{:S(2)}, u32[]{:S(2)}) async-start(bf16[8,48,2048]{2,1,0:T(8,128)(2,1)} %bitcast.76), calls=%async_computation.2 | async-start | bytes 3145728 | tf_op jit(solution)/shard_map/all_to_all | solution.py:68
  90.3 151.0 %reduce-scatter.8.cloned.1.call-start = ((), (), s32[]{:S(2)}) async-start(), calls=%async_computation.12 | async-start | bytes 3932160 | tf_op jit(solution)/shard_map/reduce_scatter | solution.py:128
  90.3 5.0 %copy-start.11 = (bf16[1,2048,768]{2,1,0:T(8,128)(2,1)S(1)}, bf16[1,2048,768]{2,1,0:T(8,128)(2,1)}, u32[]{:S(2)}) copy-start(bf16[1,2048,768]{2,1,0:T(8,128)(2,1)} %param.12) | copy-start | bytes 9437188
  94.2 1.1 copy-start.14
  116.9 0.6 copy-start.5
  116.9 0.7 copy-start.7
  116.9 0.7 copy-start.9
  116.9 1.0 copy-start.3
  121.0 35.3 %all-to-all-start.5 = ((bf16[8,48,2048]{2,1,0:T(8,128)(2,1)}), bf16[8,48,2048]{2,1,0:T(8,128)(2,1)}, u32[]{:S(2)}, u32[]{:S(2)}) async-start(bf16[8,48,2048]{2,1,0:T(8,128)(2,1)} %bitcast.73), calls=%async_computation.5 | async-start | bytes 3145728 | tf_op jit(solution)/shard_map/all_to_all | solution.py:68
  125.3 206.7 %reduce-scatter.6.cloned.1.call-start = ((), (), s32[]{:S(2)}) async-start(), calls=%async_computation.11 | async-start | bytes 3932160 | tf_op jit(solution)/shard_map/reduce_scatter | solution.py:128
  125.4 8.0 %copy-start.10 = (s32[64]{0:T(128)S(1)}, s32[64]{0:T(128)}, u32[]{:S(2)}) copy-start(s32[64]{0:T(128)} %param.14) | copy-start | bytes 772
  130.4 25.9 %collective-permute-start.1 = (bf16[384,768]{1,0:T(8,128)(2,1)}, bf16[384,768]{1,0:T(8,128)(2,1)}, u32[]{:S(2)}, u32[]{:S(2)}) collective-permute-start(bf16[384,768]{1,0:T(8,128)(2,1)} %get-tuple-element.44), channel_id=1, source_target_pairs={{0,32},{8,40},{16,48},{24,56},{32,0},{40,8},{48,16},{56,24},{1,33}... | collective-permute-start | bytes 1769480 | tf_op jit(solution)/shard_map/ppermute | solution.py:123
  165.0 25.9 %all-to-all-start.1 = ((bf16[8,48,2048]{2,1,0:T(8,128)(2,1)}), bf16[8,48,2048]{2,1,0:T(8,128)(2,1)}, u32[]{:S(2)}, u32[]{:S(2)}) async-start(bf16[8,48,2048]{2,1,0:T(8,128)(2,1)} %bitcast.77), calls=%async_computation.1 | async-start | bytes 3145728 | tf_op jit(solution)/shard_map/all_to_all | solution.py:68
  169.3 5.9 %copy-start.12 = (bf16[1,2048,768]{2,1,0:T(8,128)(2,1)S(1)}, bf16[1,2048,768]{2,1,0:T(8,128)(2,1)}, u32[]{:S(2)}) copy-start(bf16[1,2048,768]{2,1,0:T(8,128)(2,1)} %param.11) | copy-start | bytes 9437188
  169.4 5.9 %copy-start.13 = (bf16[384,768]{1,0:T(8,128)(2,1)S(1)}, bf16[384,768]{1,0:T(8,128)(2,1)}, u32[]{:S(2)}) copy-start(bf16[384,768]{1,0:T(8,128)(2,1)} %get-tuple-element.43) | copy-start | bytes 1769476
  169.4 31.0 %collective-permute-start = (bf16[384,768]{1,0:T(8,128)(2,1)}, bf16[384,768]{1,0:T(8,128)(2,1)}, u32[]{:S(2)}, u32[]{:S(2)}) collective-permute-start(bf16[384,768]{1,0:T(8,128)(2,1)} %get-tuple-element.43), channel_id=1, source_target_pairs={{0,32},{8,40},{16,48},{24,56},{32,0},{40,8},{48,16},{56,24},{1,33}... | collective-permute-start | bytes 1769480 | tf_op jit(solution)/shard_map/ppermute | solution.py:123
  190.9 25.9 %all-to-all-start.3 = ((bf16[8,48,2048]{2,1,0:T(8,128)(2,1)}), bf16[8,48,2048]{2,1,0:T(8,128)(2,1)}, u32[]{:S(2)}, u32[]{:S(2)}) async-start(bf16[8,48,2048]{2,1,0:T(8,128)(2,1)} %bitcast.75), calls=%async_computation.3 | async-start | bytes 3145728 | tf_op jit(solution)/shard_map/all_to_all | solution.py:68
  195.2 136.8 %reduce-scatter.4.cloned.1.call-start = ((), (), s32[]{:S(2)}) async-start(), calls=%async_computation.10 | async-start | bytes 3932160 | tf_op jit(solution)/shard_map/reduce_scatter | solution.py:128
  230.5 60.6 %all-to-all-start.4 = ((bf16[8,32,4224]{2,1,0:T(8,128)(2,1)}), bf16[8,32,4224]{2,1,0:T(8,128)(2,1)}, u32[]{:S(2)}, u32[]{:S(2)}) async-start(bf16[8,32,4224]{2,1,0:T(8,128)(2,1)} %bitcast.72), calls=%async_computation.4 | async-start | bytes 4325376 | tf_op jit(solution)/shard_map/all_to_all | solution.py:73
  241.3 86.3 %collective-permute-start.2 = (bf16[512,768]{1,0:T(8,128)(2,1)}, bf16[512,768]{1,0:T(8,128)(2,1)}, u32[]{:S(2)}, u32[]{:S(2)}) collective-permute-start(bf16[512,768]{1,0:T(8,128)(2,1)} %reduce-scatter.8.cloned.1.call-done), channel_id=1, source_target_pairs={{0,32},{8,40},{16,48},{24,56},{32,0},{40,8},{48,16},{56,24},{1,33}... | collective-permute-start | bytes 2359304 | tf_op jit(solution)/shard_map/ppermute | solution.py:123
  292.7 35.0 %copy-start.1 = (bf16[512,768]{1,0:T(8,128)(2,1)S(1)}, bf16[512,768]{1,0:T(8,128)(2,1)}, u32[]{:S(2)}) copy-start(bf16[512,768]{1,0:T(8,128)(2,1)} %reduce-scatter.8.cloned.1.call-done) | copy-start | bytes 2359300
Sparse Core Ops, SparseCore 0:
  11.0 43.6 all-gather.1
  117.0 36.3 reduce-scatter.7
  161.5 44.5 reduce-scatter.5
  209.1 41.4 reduce-scatter.3
